TPU v7x, 32 devices: a whole 2x2x4 slice. The times are simulated.
32 devices in a mesh: expert: 16 (over z, y, x), dp: 2 (over core).
Axes of the slice: x: 2, y: 2, z: 4, core: 2. Of those that a mesh axis runs over, the one named last changes fastest.
Arguments:
- pooled: bfloat16 [8192, 256], P(('expert', 'dp')), may hold values from -6 to 6
- routes: int32 [8192, 2], P(('expert', 'dp')), may hold values from 0 to 15, all different within a row; in each aligned block of 256 rows (0 to 255, 256 to 511, ...) at most 48 rows name the same one
- labels: int32 [8192, 2], P(('expert', 'dp')), may hold values from 0 to 1
- in_weight: bfloat16 [16, 4096, 256], P('expert'), may hold values from -0.375 to 0.375
- out_weight: bfloat16 [16, 4096, 256], P('expert'), may hold values from -0.09375 to 0.09375
- gate_weight: bfloat16 [16, 2, 256], replicated, may hold values from -0.375 to 0.375
- tower_weight: float32 [2, 256], replicated, may hold values from -0.375 to 0.375
- tower_bias: float32 [2], replicated, may hold values from -3 to 3
- bag_rows: int32 [16384], P(('expert', 'dp')), may hold values from 0 to 1023
- bag_sample: int32 [16384], P(('expert', 'dp')), may hold values from 0 to 255
- bag_weight: float32 [16384], P(('expert', 'dp')), may hold values from 0.5 to 2
- row_table: float32 [16384, 256], P('expert'), may hold values from -6 to 6
Outputs:
- in_grad: float32 [16, 4096, 256], P('expert', 'dp')
- out_grad: float32 [16, 4096, 256], P('expert', 'dp')
- gate_grad: float32 [16, 2, 256], P('expert')
- tower_grad: float32 [2, 256], replicated
- new_table: float32 [16384, 256], P('expert')
Inputs may be any that keep to these rules, and one draw needn't show every extreme that they name: `routes`: within each device's 256 rows no expert is named more than 48 times, a bound that some block reaches; a row's two experts differ.
All inputs are finite; a program needn't handle non-finite values.
Results may differ from a plain program's by a relative error of at most 0.0041.
Values may be sent and summed in bfloat16 or wider, within the bound.
A program may use at most 128 MiB of HBM per device.

v0:
```python
import jax
import jax.numpy as jnp
from jax import lax
from jax.sharding import PartitionSpec as P

LOSS_SCALE = 32.0
STEP_SIZE = 0.25
HIGH = lax.Precision.HIGHEST


def silu_grad(pre_silu):
    sigma = jax.nn.sigmoid(pre_silu)
    return sigma * (1.0 + pre_silu * (1.0 - sigma))


def route_slots(routes, owner_count, capacity):
    flat_routes = routes.reshape(-1)
    matches = flat_routes[:, None] == jnp.arange(owner_count, dtype=jnp.int32)[None, :]
    ranks = jnp.cumsum(matches.astype(jnp.int32), axis=0) - 1
    slot_of = jnp.sum(jnp.where(matches, ranks, 0), axis=1)
    return flat_routes * capacity + slot_of


def contract_first(left, right):
    return lax.dot_general(
        left, right, (((0,), (0,)), ((), ())), preferred_element_type=jnp.float32
    )


def contract_last(left, right):
    return lax.dot_general(
        left, right, (((1,), (1,)), ((), ())), preferred_element_type=jnp.float32
    )


def on_device(
    pooled,
    routes,
    labels,
    in_weight,
    out_weight,
    gate_weight,
    tower_weight,
    tower_bias,
    bag_rows,
    bag_sample,
    bag_weight,
    row_table,
):
    owner_count = lax.axis_size("expert")
    tok_rows, feature = pooled.shape
    task_count = tower_weight.shape[0]
    hidden_width = in_weight.shape[1]
    capacity = 3 * tok_rows // owner_count
    slot_index = route_slots(routes, owner_count, capacity)
    in_matrix = in_weight[0]
    out_matrix = out_weight[0]
    paired = jnp.repeat(pooled, 2, axis=0)
    outbound = jnp.zeros((owner_count * capacity, feature), jnp.bfloat16).at[slot_index].set(paired)
    outbound = outbound.reshape(owner_count, capacity, feature)
    received = lax.all_to_all(outbound, "expert", split_axis=0, concat_axis=0, tiled=True)
    sources, slot_count, _ = received.shape
    expert_inputs = received.reshape(sources * slot_count, feature)
    pre_silu = contract_last(expert_inputs, in_matrix)
    expert_hidden_act = jax.nn.silu(pre_silu).astype(jnp.bfloat16)
    result = jnp.dot(expert_hidden_act, out_matrix, preferred_element_type=jnp.float32).astype(
        jnp.bfloat16
    )
    returned = lax.all_to_all(
        result.reshape(sources, slot_count, feature),
        "expert",
        split_axis=0,
        concat_axis=0,
        tiled=True,
    )
    returned, received, pre_stack = (
        returned,
        received,
        pre_silu.reshape(sources, slot_count, hidden_width),
    )
    expert_out = (
        returned.reshape(-1, feature)[slot_index].astype(jnp.float32).reshape(tok_rows, 2, feature)
    )
    experts_all = gate_weight.shape[0]
    one_hot = (
        routes[:, :, None] == jnp.arange(experts_all, dtype=jnp.int32)[None, None, :]
    ).astype(jnp.float32)
    gate_flat = gate_weight.reshape(experts_all * task_count, feature)
    all_logits = contract_last(pooled, gate_flat).reshape(tok_rows, experts_all, task_count)
    chosen = jnp.einsum("nke,net->ntk", one_hot, all_logits, precision=HIGH)
    gate_first = jax.nn.sigmoid(chosen[:, :, 0] - chosen[:, :, 1])
    gate_second = 1.0 - gate_first
    mixture = (
        gate_first[:, :, None] * expert_out[:, None, 0, :]
        + gate_second[:, :, None] * expert_out[:, None, 1, :]
    )
    task_logit = jnp.sum(mixture * tower_weight[None], axis=2) + tower_bias[None]
    logit_grad = LOSS_SCALE * (jax.nn.sigmoid(task_logit) - labels.astype(jnp.float32))
    tower_local = jnp.einsum("nt,ntf->tf", logit_grad, mixture, precision=HIGH)
    mixture_grad = logit_grad[:, :, None] * tower_weight[None]
    routed_grad = jnp.stack(
        [
            jnp.sum(gate_first[:, :, None] * mixture_grad, axis=1),
            jnp.sum(gate_second[:, :, None] * mixture_grad, axis=1),
        ],
        axis=1,
    ).astype(jnp.bfloat16)
    gate_dot = jnp.einsum("ntf,nkf->ntk", mixture_grad, expert_out, precision=HIGH)
    first_grad = (gate_dot[:, :, 0] - gate_dot[:, :, 1]) * gate_first * gate_second
    select_grad = jnp.stack([first_grad, -first_grad], axis=2)
    mix_table = jnp.einsum("nke,ntk->net", one_hot, select_grad, precision=HIGH).reshape(
        tok_rows, experts_all * task_count
    )
    gate_local = lax.dot_general(
        mix_table, pooled.astype(jnp.float32), (((0,), (0,)), ((), ())), precision=HIGH
    ).reshape(experts_all, task_count, feature)
    gate_input = jnp.dot(mix_table, gate_flat.astype(jnp.float32), precision=HIGH)
    grad_outbound = (
        jnp.zeros((owner_count * capacity, feature), jnp.bfloat16)
        .at[slot_index]
        .set(routed_grad.reshape(tok_rows * 2, feature))
    )
    grad_received = lax.all_to_all(
        grad_outbound.reshape(owner_count, capacity, feature),
        "expert",
        split_axis=0,
        concat_axis=0,
        tiled=True,
    )
    inputs = received.reshape(-1, feature)
    grad_rows = grad_received.reshape(-1, feature)
    pre_silu = pre_stack.reshape(-1, hidden_width)
    hidden_act = jax.nn.silu(pre_silu).astype(jnp.bfloat16)
    hidden_grad = contract_last(grad_rows, out_matrix)
    pre_grad = (hidden_grad * silu_grad(pre_silu)).astype(jnp.bfloat16)
    input_rows = jnp.dot(pre_grad, in_matrix, preferred_element_type=jnp.float32).astype(
        jnp.bfloat16
    )
    grad_back = lax.all_to_all(
        input_rows.reshape(owner_count, capacity, feature),
        "expert",
        split_axis=0,
        concat_axis=0,
        tiled=True,
    )
    input_grad = (
        grad_back.reshape(-1, feature)[slot_index].astype(jnp.float32).reshape(tok_rows, 2, feature)
    )
    pooled_grad = gate_input + input_grad[:, 0] + input_grad[:, 1]
    per_owner = bag_rows.shape[0] // owner_count
    row_grads = (
        (bag_weight[:, None] * pooled_grad[bag_sample])
        .astype(jnp.bfloat16)
        .reshape(owner_count, per_owner, feature)
    )
    owned_grads, owned_rows = (
        lax.all_to_all(row_grads, "expert", split_axis=0, concat_axis=0, tiled=True),
        lax.all_to_all(
            bag_rows.reshape(owner_count, per_owner),
            "expert",
            split_axis=0,
            concat_axis=0,
            tiled=True,
        ),
    )
    table_size = row_table.shape[0]
    summed = lax.psum_scatter(
        jnp.concatenate(
            [contract_first(pre_grad, inputs), contract_first(hidden_act, grad_rows)], axis=1
        ),
        "dp",
        scatter_dimension=0,
        tiled=True,
    )
    in_grad = summed[:, :feature][None]
    out_grad = summed[:, feature:][None]
    gate_total, tower_grad = lax.psum((gate_local, tower_local), ("expert", "dp"))
    gate_grad = lax.dynamic_slice_in_dim(gate_total, lax.axis_index("expert"), 1, 0)
    matches = (
        owned_rows.reshape(-1)[:, None] == jnp.arange(table_size, dtype=jnp.int32)[None, :]
    ).astype(jnp.bfloat16)
    row_sums = lax.psum(contract_first(matches, owned_grads.reshape(-1, feature)), "dp")
    new_table = row_table - STEP_SIZE * row_sums
    return (in_grad, out_grad, gate_grad, tower_grad, new_table)


def solution(mesh):
    in_specs = (
        P(("expert", "dp"), None),
        P(("expert", "dp"), None),
        P(("expert", "dp"), None),
        P("expert", None, None),
        P("expert", None, None),
        P(),
        P(),
        P(),
        P(("expert", "dp")),
        P(("expert", "dp")),
        P(("expert", "dp")),
        P("expert", None),
    )
    out_specs = (
        P("expert", "dp", None),
        P("expert", "dp", None),
        P("expert", None, None),
        P(),
        P("expert", None),
    )
    return jax.shard_map(
        on_device, mesh=mesh, in_specs=in_specs, out_specs=out_specs, check_vma=False
    )
```

profile of v0, /device:TPU:0, one launch (start us, length us, event | category | flops | bytes accessed | tf_op | source)
XLA Modules:
  0.0 216.7 jit_solution(16531580779659495678)
XLA Ops:
  7.2 0.8 broadcast_multiply_fusion
  8.0 0.8 copy.107
  9.4 1.2 reduce-window.6
  10.6 0.2 slice_reduce_fusion
  10.8 1.1 broadcast_in_dim.13
  12.1 3.1 %scatter_custom_fusion = bf16[768,256]{1,0:T(8,128)(2,1)} fusion(s32[512]{0:T(512)S(1)} %bitcast.112, bf16[512,256]{1,0:T(8,128)(2,1)S(1)} %reshape.166, bf16[]{:T(256)} %constant.13.clone.1), kind=kCustom, calls=%fused_computation.51 | custom fusion | bytes 393218 | tf_op jit(solution)/shard_map/scatter | solution.py:59
  15.2 8.3 %all-to-all-start = ((bf16[16,48,256]{2,1,0:T(8,128)(2,1)}), bf16[16,48,256]{2,1,0:T(8,128)(2,1)S(1)}, u32[]{:S(2)}, u32[]{:S(2)}) async-start(bf16[16,48,256]{2,1,0:T(8,128)(2,1)} %bitcast.5), calls=%async_computation | async-start | bytes 786432 | tf_op jit(solution)/shard_map/all_to_all | solution.py:61
  23.5 1.1 fusion.34
  24.6 0.2 copy.112
  24.8 11.4 %all-to-all-done = bf16[16,48,256]{2,1,0:T(8,128)(2,1)S(1)} async-done(((bf16[16,48,256]{2,1,0:T(8,128)(2,1)}), bf16[16,48,256]{2,1,0:T(8,128)(2,1)S(1)}, u32[]{:S(2)}, u32[]{:S(2)}) %all-to-all-start) | async-done | bytes 393248 | tf_op jit(solution)/shard_map/all_to_all | solution.py:61
  36.1 6.5 %multiply_convert_fusion.1 = (bf16[768,4096]{1,0:T(8,128)(2,1)S(1)}, f32[768,4096]{1,0:T(8,128)}) fusion(bf16[768,256]{1,0:T(8,128)(2,1)S(1)} %bitcast.101, bf16[1,4096,256]{2,1,0:T(8,128)(2,1)S(1)} %copy-done), kind=kOutput, calls=%fused_computation.6 | convolution fusion | flops 1626341376 | bytes 21364736 | tf_op jit(solution)/shard_map/dot_general | solution.py:31
  42.6 2.6 %copy-done.2 = bf16[768,4096]{1,0:T(8,128)(2,1)} copy-done((bf16[768,4096]{1,0:T(8,128)(2,1)}, bf16[768,4096]{1,0:T(8,128)(2,1)S(1)}, u32[]{:S(2)}) %copy-start.2) | copy-done | bytes 6291480
  45.2 2.5 %fusion.11 = bf16[768,256]{1,0:T(8,128)(2,1)} fusion(bf16[768,4096]{1,0:T(8,128)(2,1)S(1)} %get-tuple-element.55, bf16[1,4096,256]{2,1,0:T(8,128)(2,1)S(1)} %copy-done.23), kind=kOutput, calls=%fused_computation.21 | convolution fusion | flops 1610809344 | bytes 8781824 | tf_op jit(solution)/shard_map/dot_general | solution.py:66
  47.8 3.7 %all-to-all-start.1 = ((bf16[16,48,256]{2,1,0:T(8,128)(2,1)}), bf16[16,48,256]{2,1,0:T(8,128)(2,1)S(1)}, u32[]{:S(2)}, u32[]{:S(2)}) async-start(bf16[16,48,256]{2,1,0:T(8,128)(2,1)} %bitcast.9), calls=%async_computation.1 | async-start | bytes 786432 | tf_op jit(solution)/shard_map/all_to_all | solution.py:69
  51.5 1.1 fusion.27
  52.6 0.2 fusion.50
  53.3 0.7 all_to_all.24
  54.0 9.5 %all-to-all-done.1 = bf16[16,48,256]{2,1,0:T(8,128)(2,1)S(1)} async-done(((bf16[16,48,256]{2,1,0:T(8,128)(2,1)}), bf16[16,48,256]{2,1,0:T(8,128)(2,1)S(1)}, u32[]{:S(2)}, u32[]{:S(2)}) %all-to-all-start.1) | async-done | bytes 393248 | tf_op jit(solution)/shard_map/all_to_all | solution.py:69
  63.6 3.7 %all-to-all-start.3 = ((s32[16,1,32]{2,1,0:T(1,128)}), s32[16,1,32]{2,1,0:T(1,128)S(1)}, u32[]{:S(2)}, u32[]{:S(2)}) async-start(s32[16,1,32]{2,1,0:T(1,128)} %all_to_all.24), calls=%async_computation.4 | async-start | bytes 16384 | tf_op jit(solution)/shard_map/all_to_all | solution.py:158
  67.3 2.0 gather_fusion
  69.3 0.4 fusion.49
  69.8 1.2 multiply_reduce_fusion
  71.3 1.6 fusion.19
  72.9 1.0 copy.119
  73.9 1.1 reshape.174
  74.9 3.1 %scatter_custom_fusion.1 = bf16[768,256]{1,0:T(8,128)(2,1)} fusion(s32[512]{0:T(512)S(1)} %bitcast.114, bf16[512,256]{1,0:T(8,128)(2,1)S(1)} %reshape.174, bf16[]{:T(256)} %constant.13.clone.1), kind=kCustom, calls=%fused_computation.49 | custom fusion | bytes 393218 | tf_op jit(solution)/shard_map/scatter | solution.py:121
  78.0 0.6 copy-done.10
  78.6 6.8 %all-to-all-start.2 = ((bf16[16,48,256]{2,1,0:T(8,128)(2,1)}), bf16[16,48,256]{2,1,0:T(8,128)(2,1)S(1)}, u32[]{:S(2)}, u32[]{:S(2)}) async-start(bf16[16,48,256]{2,1,0:T(8,128)(2,1)} %bitcast.14), calls=%async_computation.2 | async-start | bytes 786432 | tf_op jit(solution)/shard_map/all_to_all | solution.py:123
  85.5 0.8 mul.155
  86.2 0.7 compare_select_fusion.1
  86.9 0.6 pad_clamp_fusion
  87.5 0.5 broadcast.113
  88.0 1.3 reduce.5
  89.3 0.7 eq.64
  90.0 2.7 %fusion.17 = f32[256,2,2]{1,2,0:T(2,128)} fusion(bf16[256,2,256]{2,1,0:T(2,128)(2,1)S(1)} %gather.14, f32[256,2]{1,0:T(8,128)S(1)} %copy.118, f32[2,256]{1,0:T(2,128)} %param.18), kind=kOutput, calls=%fused_computation.27 | convolution fusion | flops 3276800 | bytes 270336 | tf_op jit(solution)/shard_map/ntf,nkf->ntk/dot_general | solution.py:108
  92.6 3.9 %all-to-all-done.2 = bf16[16,48,256]{2,1,0:T(8,128)(2,1)S(1)} async-done(((bf16[16,48,256]{2,1,0:T(8,128)(2,1)}), bf16[16,48,256]{2,1,0:T(8,128)(2,1)S(1)}, u32[]{:S(2)}, u32[]{:S(2)}) %all-to-all-start.2) | async-done | bytes 393248 | tf_op jit(solution)/shard_map/all_to_all | solution.py:123
  96.6 8.8 %multiply_convert_fusion = bf16[768,4096]{1,0:T(8,128)(2,1)S(1)} fusion(f32[768,4096]{1,0:T(8,128)} %get-tuple-element.56, bf16[768,256]{1,0:T(8,128)(2,1)S(1)} %bitcast.103, bf16[1,4096,256]{2,1,0:T(8,128)(2,1)} %param.16), kind=kOutput, calls=%fused_computation.5 | convolution fusion | flops 1638924288 | bytes 21364736 | tf_op jit(solution)/shard_map/dot_general | solution.py:31
  105.3 2.7 %copy-done.3 = bf16[768,4096]{1,0:T(8,128)(2,1)} copy-done((bf16[768,4096]{1,0:T(8,128)(2,1)}, bf16[768,4096]{1,0:T(8,128)(2,1)S(1)}, u32[]{:S(2)}) %copy-start.3) | copy-done | bytes 6291480
  108.0 2.5 %fusion.8 = bf16[768,256]{1,0:T(8,128)(2,1)} fusion(bf16[768,4096]{1,0:T(8,128)(2,1)S(1)} %multiply_convert_fusion, bf16[1,4096,256]{2,1,0:T(8,128)(2,1)S(1)} %copy-done), kind=kOutput, calls=%fused_computation.20 | convolution fusion | flops 1610809344 | bytes 8781824 | tf_op jit(solution)/shard_map/dot_general | solution.py:136
  110.5 3.9 %all-to-all-start.4 = ((bf16[16,48,256]{2,1,0:T(8,128)(2,1)}), bf16[16,48,256]{2,1,0:T(8,128)(2,1)S(1)}, u32[]{:S(2)}, u32[]{:S(2)}) async-start(bf16[16,48,256]{2,1,0:T(8,128)(2,1)} %bitcast.107), calls=%async_computation.5 | async-start | bytes 786432 | tf_op jit(solution)/shard_map/all_to_all | solution.py:139
  114.5 1.3 fusion.48
  116.1 1.8 fusion.26
  117.9 7.9 %all-to-all-done.4 = bf16[16,48,256]{2,1,0:T(8,128)(2,1)S(1)} async-done(((bf16[16,48,256]{2,1,0:T(8,128)(2,1)}), bf16[16,48,256]{2,1,0:T(8,128)(2,1)S(1)}, u32[]{:S(2)}, u32[]{:S(2)}) %all-to-all-start.4) | async-done | bytes 393248 | tf_op jit(solution)/shard_map/all_to_all | solution.py:139
  125.8 1.9 gather_fusion.1
  127.8 0.3 reshape.137
  128.0 0.4 fusion.47
  128.5 1.3 fusion.15
  129.8 1.6 gather_fusion.2
  131.3 0.8 multiply_convert_fusion.2
  132.2 3.6 %all-to-all-start.5 = ((bf16[16,32,256]{2,1,0:T(8,128)(2,1)}), bf16[16,32,256]{2,1,0:T(8,128)(2,1)S(1)}, u32[]{:S(2)}, u32[]{:S(2)}) async-start(bf16[16,32,256]{2,1,0:T(8,128)(2,1)} %multiply_convert_fusion.2), calls=%async_computation.6 | async-start | bytes 524288 | tf_op jit(solution)/shard_map/all_to_all | solution.py:157
  135.9 6.7 %fusion.52 = f32[4096,256]{0,1:T(8,128)} fusion(bf16[768,4096]{1,0:T(8,128)(2,1)} %copy-done.2, bf16[768,256]{1,0:T(8,128)(2,1)} %bitcast.104), kind=kOutput, calls=%fused_computation.92 | convolution fusion | flops 1610612736 | bytes 10878976 | tf_op jit(solution)/shard_map/dot_general | solution.py:25
  142.6 2.1 all-to-all-done.5
  144.7 1.8 fusion.7
  146.6 4.8 %fusion.51 = f32[4096,256]{0,1:T(8,128)S(1)} fusion(bf16[768,4096]{1,0:T(8,128)(2,1)} %copy-done.3, bf16[768,256]{1,0:T(8,128)(2,1)S(1)} %bitcast.102), kind=kOutput, calls=%fused_computation.91 | convolution fusion | flops 1610612736 | bytes 10878976 | tf_op jit(solution)/shard_map/dot_general | solution.py:25
  151.4 3.8 %pad_maximum_fusion = f32[4096,512]{0,1:T(8,128)} fusion(f32[4096,256]{0,1:T(8,128)S(1)} %copy-done.1, f32[4096,256]{0,1:T(8,128)S(1)} %fusion.51), kind=kLoop, calls=%fused_computation.8 | loop fusion | flops 2097152 | bytes 16777216 | tf_op jit(solution)/shard_map/concatenate | solution.py:168
  155.2 0.9 copy-done.8
  156.3 0.4 fusion.21
  156.7 0.2 fusion.32
  156.9 39.3 %all-reduce = (f32[16,2,256]{2,0,1:T(8,128)S(1)}, f32[2,256]{1,0:T(2,128)}) all-reduce(f32[16,2,256]{2,0,1:T(8,128)S(1)} %fusion.32, f32[2,256]{1,0:T(2,128)S(1)} %bitcast.116), channel_id=1, replica_groups=mesh['expert'=16,'dp'=2] {'expert','dp'}, use_global_device_ids=true, to_apply=%region_9.10 | all-reduce | flops 8704 | bytes 69632 | tf_op jit(solution)/shard_map/psum | solution.py:177
  196.2 0.6 copy.131
  196.8 2.6 %multiply_subtract_fusion = f32[1024,256]{1,0:T(8,128)} fusion(f32[1024,256]{1,0:T(8,128)} %param.23, f32[1024,256]{1,0:T(8,128)} %all-reduce.3.cloned.1.call-done), kind=kLoop, calls=%fused_computation.25 | loop fusion | flops 524288 | bytes 3145728 | tf_op jit(solution)/shard_map/sub | solution.py:183
  199.4 4.7 %slice_bitcast_fusion = (f32[1,2048,256]{1,2,0:T(8,128)}, f32[1,2048,256]{1,2,0:T(8,128)}) fusion(f32[2048,512]{0,1:T(8,128)} %reduce-scatter.2.cloned.1.call-done), kind=kLoop, calls=%fused_computation.9 | loop fusion | bytes 8388608 | tf_op jit(solution)/shard_map/broadcast_in_dim | solution.py:176
  204.1 2.9 %copy.129 = f32[1,2048,256]{2,1,0:T(8,128)} copy(f32[1,2048,256]{1,2,0:T(8,128)} %get-tuple-element.46) | data formatting | bytes 4194304
  207.0 2.9 %copy.130 = f32[1,2048,256]{2,1,0:T(8,128)} copy(f32[1,2048,256]{1,2,0:T(8,128)} %get-tuple-element.45) | data formatting | bytes 4194304
  (83 shorter events, 2.5 us)
Async XLA Ops:
  7.2 29.0 %copy-start = (bf16[1,4096,256]{2,1,0:T(8,128)(2,1)S(1)}, bf16[1,4096,256]{2,1,0:T(8,128)(2,1)}, u32[]{:S(2)}) copy-start(bf16[1,4096,256]{2,1,0:T(8,128)(2,1)} %param.15) | copy-start | bytes 6291460
  15.2 21.0 %all-to-all-start = ((bf16[16,48,256]{2,1,0:T(8,128)(2,1)}), bf16[16,48,256]{2,1,0:T(8,128)(2,1)S(1)}, u32[]{:S(2)}, u32[]{:S(2)}) async-start(bf16[16,48,256]{2,1,0:T(8,128)(2,1)} %bitcast.5), calls=%async_computation | async-start | bytes 786432 | tf_op jit(solution)/shard_map/all_to_all | solution.py:61
  36.1 6.5 %copy-start.4 = (bf16[16,48,256]{2,1,0:T(8,128)(2,1)}, bf16[16,48,256]{2,1,0:T(8,128)(2,1)S(1)}, u32[]{:S(2)}) copy-start(bf16[16,48,256]{2,1,0:T(8,128)(2,1)S(1)} %all-to-all-done) | copy-start | bytes 1179652
  36.1 9.1 %copy-start.23 = (bf16[1,4096,256]{2,1,0:T(8,128)(2,1)S(1)}, bf16[1,4096,256]{2,1,0:T(8,128)(2,1)}, u32[]{:S(2)}) copy-start(bf16[1,4096,256]{2,1,0:T(8,128)(2,1)} %param.16) | copy-start | bytes 6291460
  42.6 2.6 %copy-start.2 = (bf16[768,4096]{1,0:T(8,128)(2,1)}, bf16[768,4096]{1,0:T(8,128)(2,1)S(1)}, u32[]{:S(2)}) copy-start(bf16[768,4096]{1,0:T(8,128)(2,1)S(1)} %get-tuple-element.55) | copy-start | bytes 18874372
  45.2 8.1 %copy-start.19 = (s32[512]{0:T(512)S(1)}, s32[512]{0:T(512)}, u32[]{:S(2)}) copy-start(s32[512]{0:T(512)} %param.20) | copy-start | bytes 6148
  47.8 22.0 %copy-start.18 = (f32[2,256]{1,0:T(2,128)S(1)}, f32[2,256]{1,0:T(2,128)}, u32[]{:S(2)}) copy-start(f32[2,256]{1,0:T(2,128)} %param.18) | copy-start | bytes 6148
  47.8 23.3 %copy-start.21 = (s32[256,2]{0,1:T(2,128)S(1)}, s32[256,2]{0,1:T(2,128)}, u32[]{:S(2)}) copy-start(s32[256,2]{0,1:T(2,128)} %param.14) | copy-start | bytes 6148
  47.8 23.3 %copy-start.22 = (f32[2]{0:T(128)S(1)}, f32[2]{0:T(128)}, u32[]{:S(2)}) copy-start(f32[2]{0:T(128)} %param.19) | copy-start | bytes 28
  47.8 15.8 %all-to-all-start.1 = ((bf16[16,48,256]{2,1,0:T(8,128)(2,1)}), bf16[16,48,256]{2,1,0:T(8,128)(2,1)S(1)}, u32[]{:S(2)}, u32[]{:S(2)}) async-start(bf16[16,48,256]{2,1,0:T(8,128)(2,1)} %bitcast.9), calls=%async_computation.1 | async-start | bytes 786432 | tf_op jit(solution)/shard_map/all_to_all | solution.py:69
  53.0 14.2 %copy-start.13 = (f32[256,2,1]{0,1,2:T(2,128)}, f32[256,2,1]{0,1,2:T(2,128)S(1)}, u32[]{:S(2)}) copy-start(f32[256,2,1]{0,1,2:T(2,128)S(1)} %get-tuple-element.44) | copy-start | bytes 6148
  54.0 15.7 %copy-start.15 = (s32[1024]{0:T(1024)}, s32[1024]{0:T(1024)S(1)}, u32[]{:S(2)}) copy-start(s32[1024]{0:T(1024)S(1)} %pad_clamp_fusion.1) | copy-start | bytes 12292
  63.6 14.4 %all-to-all-start.3 = ((s32[16,1,32]{2,1,0:T(1,128)}), s32[16,1,32]{2,1,0:T(1,128)S(1)}, u32[]{:S(2)}, u32[]{:S(2)}) async-start(s32[16,1,32]{2,1,0:T(1,128)} %all_to_all.24), calls=%async_computation.4 | async-start | bytes 16384 | tf_op jit(solution)/shard_map/all_to_all | solution.py:158
  71.1 1.7 copy-start.11
  78.0 0.6 copy-start.10
  78.6 18.0 %all-to-all-start.2 = ((bf16[16,48,256]{2,1,0:T(8,128)(2,1)}), bf16[16,48,256]{2,1,0:T(8,128)(2,1)S(1)}, u32[]{:S(2)}, u32[]{:S(2)}) async-start(bf16[16,48,256]{2,1,0:T(8,128)(2,1)} %bitcast.14), calls=%async_computation.2 | async-start | bytes 786432 | tf_op jit(solution)/shard_map/all_to_all | solution.py:123
  96.6 8.8 %copy-start.6 = (bf16[16,48,256]{2,1,0:T(8,128)(2,1)}, bf16[16,48,256]{2,1,0:T(8,128)(2,1)S(1)}, u32[]{:S(2)}) copy-start(bf16[16,48,256]{2,1,0:T(8,128)(2,1)S(1)} %all-to-all-done.2) | copy-start | bytes 1179652
  105.3 2.7 %copy-start.3 = (bf16[768,4096]{1,0:T(8,128)(2,1)}, bf16[768,4096]{1,0:T(8,128)(2,1)S(1)}, u32[]{:S(2)}) copy-start(bf16[768,4096]{1,0:T(8,128)(2,1)S(1)} %multiply_convert_fusion) | copy-start | bytes 18874372
  108.0 7.9 %copy-start.14 = (f32[256,2,1]{0,1,2:T(2,128)S(1)}, f32[256,2,1]{0,1,2:T(2,128)}, u32[]{:S(2)}) copy-start(f32[256,2,1]{0,1,2:T(2,128)} %copy-done.13) | copy-start | bytes 6148
  108.0 17.8 %copy-start.16 = (s32[1024]{0:T(1024)S(1)}, s32[1024]{0:T(1024)}, u32[]{:S(2)}) copy-start(s32[1024]{0:T(1024)} %copy-done.15) | copy-start | bytes 12292
  110.5 17.9 %copy-start.9 = (bf16[16,2,256]{2,1,0:T(2,128)(2,1)S(1)}, bf16[16,2,256]{2,1,0:T(2,128)(2,1)}, u32[]{:S(2)}) copy-start(bf16[16,2,256]{2,1,0:T(2,128)(2,1)} %param.17) | copy-start | bytes 49156
  110.5 19.2 %copy-start.17 = (s32[1024]{0:T(1024)S(1)}, s32[1024]{0:T(1024)}, u32[]{:S(2)}) copy-start(s32[1024]{0:T(1024)} %pad_clamp_fusion) | copy-start | bytes 12292
  110.5 15.3 %all-to-all-start.4 = ((bf16[16,48,256]{2,1,0:T(8,128)(2,1)}), bf16[16,48,256]{2,1,0:T(8,128)(2,1)S(1)}, u32[]{:S(2)}, u32[]{:S(2)}) async-start(bf16[16,48,256]{2,1,0:T(8,128)(2,1)} %bitcast.107), calls=%async_computation.5 | async-start | bytes 786432 | tf_op jit(solution)/shard_map/all_to_all | solution.py:139
  132.2 12.5 %all-to-all-start.5 = ((bf16[16,32,256]{2,1,0:T(8,128)(2,1)}), bf16[16,32,256]{2,1,0:T(8,128)(2,1)S(1)}, u32[]{:S(2)}, u32[]{:S(2)}) async-start(bf16[16,32,256]{2,1,0:T(8,128)(2,1)} %multiply_convert_fusion.2), calls=%async_computation.6 | async-start | bytes 524288 | tf_op jit(solution)/shard_map/all_to_all | solution.py:157
  135.8 8.9 %copy-start.20 = (s32[512]{0:T(512)S(1)}, s32[512]{0:T(512)}, u32[]{:S(2)}) copy-start(s32[512]{0:T(512)} %eq.64) | copy-start | bytes 6148
  135.8 10.7 %copy-start.5 = (bf16[16,48,256]{2,1,0:T(8,128)(2,1)S(1)}, bf16[16,48,256]{2,1,0:T(8,128)(2,1)}, u32[]{:S(2)}) copy-start(bf16[16,48,256]{2,1,0:T(8,128)(2,1)} %copy-done.4) | copy-start | bytes 1179652
  135.8 60.9 %all-reduce.3.cloned.1.call-start = ((), (), s32[]{:S(2)}) async-start(), calls=%async_computation.8 | async-start | bytes 2097152 | tf_op jit(solution)/shard_map/psum | solution.py:182
  146.5 52.9 %reduce-scatter.2.cloned.1.call-start = ((), (), s32[]{:S(2)}) async-start(), calls=%async_computation.7 | async-start | bytes 12582912 | tf_op jit(solution)/shard_map/reduce_scatter | solution.py:167
  146.6 4.8 %copy-start.1 = (f32[4096,256]{0,1:T(8,128)S(1)}, f32[4096,256]{0,1:T(8,128)}, u32[]{:S(2)}) copy-start(f32[4096,256]{0,1:T(8,128)} %fusion.52) | copy-start | bytes 12582916
  155.2 0.9 copy-start.8
  155.2 1.1 copy-start.12
  155.2 1.5 copy-start.7
Sparse Core Ops, SparseCore 0:
  146.6 18.6 all-reduce.2
  167.6 17.4 reduce-scatter.1
where the time goes:
time: 218 us; the launch traced here: 217 us
  matrix products  42.1 us (19%)
  local copies, waits for them, and re-layouts  40.9 us (19%)
  blocking collectives  39.3 us (18%)
  waiting for transfers between devices  34.8 us (16%)
  starting transfers between devices  30.2 us (14%)
  other arithmetic  14.8 us (7%)
  between operations  14.5 us (7%)
    psum x1, blocking collectives, on_device(): lax.psum((gate_local, tower_local), ('expert', 'dp'))  39.3 us
    dot_general x3, matrix products, contract_last(): lax.dot_general(left, right, (((1,), (1,)), ((), ())), preferred_element_...  16.3 us
    unnamed x57, local copies, waits for them, and re-layouts  14.4 us
    dot_general x3, matrix products, contract_first(): lax.dot_general(left, right, (((0,), (0,)), ((), ())), preferred_element_...  13.3 us
    all_to_all x1, waiting for transfers between devices, on_device(): lax.all_to_all(outbound, 'expert', split_axis=0, concat_axis=0, tiled=True)  11.4 us
    all_to_all x1, waiting for transfers between devices, on_device(): lax.all_to_all(result.reshape(sources, slot_count, feature), 'expert', sp...  9.54 us
    all_to_all x1, starting transfers between devices, on_device(): lax.all_to_all(outbound, 'expert', split_axis=0, concat_axis=0, tiled=True)  8.34 us
    all_to_all x1, waiting for transfers between devices, on_device(): lax.all_to_all(input_rows.reshape(owner_count, capacity, feature), 'exper...  7.88 us
  transfers between devices with their start and end apart: 8, of which 5 were waited for; matrix products, arithmetic and copies ran while one was open for 20% of the time, Pallas kernels for 0%

commit v1 on v0

v1 whole, which is shorter than its diff:
```python
import jax
import jax.numpy as jnp
from jax import lax
from jax.sharding import PartitionSpec as P

LOSS_SCALE = 32.0
STEP_SIZE = 0.25
HIGH = lax.Precision.HIGHEST


def silu_grad(pre_silu):
    sigma = jax.nn.sigmoid(pre_silu)
    return sigma * (1.0 + pre_silu * (1.0 - sigma))


def contract_first(left, right):
    return lax.dot_general(
        left, right, (((0,), (0,)), ((), ())), preferred_element_type=jnp.float32
    )


def contract_last(left, right):
    return lax.dot_general(
        left, right, (((1,), (1,)), ((), ())), preferred_element_type=jnp.float32
    )


def on_device(
    pooled,
    routes,
    labels,
    in_weight,
    out_weight,
    gate_weight,
    tower_weight,
    tower_bias,
    bag_rows,
    bag_sample,
    bag_weight,
    row_table,
):
    owner_count = lax.axis_size("expert")
    tok_rows, feature = pooled.shape
    task_count = tower_weight.shape[0]
    capacity = 3 * tok_rows // owner_count
    in_matrix = in_weight[0]
    out_matrix = out_weight[0]
    experts = jnp.arange(owner_count, dtype=jnp.int32)[None, :]
    match_first = (routes[:, :1] == experts).astype(jnp.float32)
    match_second = (routes[:, 1:] == experts).astype(jnp.float32)
    before = jnp.tril(jnp.ones((tok_rows, tok_rows), jnp.float32), -1)
    ranks = jnp.dot(before, jnp.concatenate([match_first, match_second], axis=1))
    rank_first = ranks[:, :owner_count]
    rank_second = ranks[:, owner_count:] + jnp.sum(match_first, axis=0)[None]
    slot_first = jnp.sum(match_first * rank_first, axis=1).astype(jnp.int32) + routes[:, 0] * capacity
    slot_second = jnp.sum(match_second * rank_second, axis=1).astype(jnp.int32) + routes[:, 1] * capacity
    places = jnp.arange(owner_count * capacity, dtype=jnp.int32)[None, :]
    at_first = (slot_first[:, None] == places).astype(jnp.bfloat16)
    at_second = (slot_second[:, None] == places).astype(jnp.bfloat16)
    at_both = at_first + at_second

    def swap(values):
        return lax.all_to_all(values, "expert", split_axis=0, concat_axis=0, tiled=True)

    outbound = contract_first(at_both, pooled).astype(jnp.bfloat16)
    inputs = swap(outbound.reshape(owner_count, capacity, feature)).reshape(-1, feature)
    tower_out = lax.dot_general(
        tower_weight, out_matrix.astype(jnp.float32), (((1,), (1,)), ((), ())), precision=HIGH
    )
    pre_silu = contract_last(inputs, in_matrix)
    hidden_act = jax.nn.silu(pre_silu).astype(jnp.bfloat16)
    hidden_f32 = hidden_act.astype(jnp.float32)
    dots = lax.dot_general(
        tower_out, hidden_f32, (((1,), (1,)), ((), ())), precision=lax.Precision.HIGH
    )
    dots = dots.reshape(task_count, owner_count, capacity).transpose(1, 0, 2)
    dots = swap(dots).transpose(1, 0, 2).reshape(task_count, -1)
    dot_first = lax.dot_general(at_first.astype(jnp.float32), dots, (((1,), (1,)), ((), ())), precision=HIGH)
    dot_second = lax.dot_general(at_second.astype(jnp.float32), dots, (((1,), (1,)), ((), ())), precision=HIGH)
    gate_flat = gate_weight.reshape(-1, feature)
    all_logits = contract_last(pooled, gate_flat).reshape(tok_rows, owner_count, task_count)
    gate_first = jax.nn.sigmoid(
        jnp.sum((match_first - match_second)[:, :, None] * all_logits, axis=1)
    )
    gate_second = 1.0 - gate_first
    task_logit = gate_first * dot_first + gate_second * dot_second + tower_bias[None]
    logit_grad = LOSS_SCALE * (jax.nn.sigmoid(task_logit) - labels.astype(jnp.float32))
    first_grad = logit_grad * (dot_first - dot_second) * gate_first * gate_second
    scalars_first = jnp.concatenate([gate_first * logit_grad, first_grad], axis=1)
    scalars_second = jnp.concatenate([gate_second * logit_grad, -first_grad], axis=1)
    sent = lax.dot_general(
        scalars_first, at_first.astype(jnp.float32), (((0,), (0,)), ((), ())), precision=HIGH
    ) + lax.dot_general(
        scalars_second, at_second.astype(jnp.float32), (((0,), (0,)), ((), ())), precision=HIGH
    )
    sent = sent.reshape(2 * task_count, owner_count, capacity).transpose(1, 0, 2)
    scalars = swap(sent).transpose(1, 0, 2).reshape(2 * task_count, -1)
    coefs = scalars[:task_count]
    hidden_grad = sum(coefs[t][:, None] * tower_out[t][None, :] for t in range(task_count))
    pre_grad = (hidden_grad * silu_grad(pre_silu)).astype(jnp.bfloat16)
    input_rows = jnp.dot(pre_grad, in_matrix, preferred_element_type=jnp.float32).astype(jnp.bfloat16)
    mix_table = (
        (match_first - match_second)[:, :, None] * first_grad[:, None, :]
    ).reshape(tok_rows, owner_count * task_count)
    gate_input = jnp.dot(mix_table, gate_flat.astype(jnp.float32), precision=HIGH)
    back = swap(input_rows.reshape(owner_count, capacity, feature)).reshape(-1, feature)
    pooled_grad = gate_input + jnp.dot(at_both, back, preferred_element_type=jnp.float32)
    per_owner = bag_rows.shape[0] // owner_count
    row_grads = (bag_weight[:, None] * pooled_grad[bag_sample]).astype(jnp.bfloat16)
    owned_grads = swap(row_grads.reshape(owner_count, per_owner, feature))
    owned_rows = swap(bag_rows.reshape(owner_count, per_owner))
    hidden_sum = jnp.dot(coefs, hidden_f32, precision=lax.Precision.HIGH)
    in_grad = lax.psum_scatter(
        contract_first(pre_grad, inputs), "dp", scatter_dimension=0, tiled=True
    )
    gate_local = jnp.dot(scalars[task_count:], inputs.astype(jnp.float32), precision=HIGH)
    tower_local = jnp.dot(hidden_sum, out_matrix.astype(jnp.float32), precision=HIGH)
    tower_grad = lax.psum(tower_local, ("expert", "dp"))
    gate_grad = lax.psum(gate_local, "dp")
    hidden_mine = lax.psum_scatter(hidden_sum, "dp", scatter_dimension=1, tiled=True)
    out_grad = sum(hidden_mine[t][:, None] * tower_weight[t][None, :] for t in range(task_count))
    table_size = row_table.shape[0]
    matches = (
        owned_rows.reshape(-1)[:, None] == jnp.arange(table_size, dtype=jnp.int32)[None, :]
    ).astype(jnp.bfloat16)
    row_sums = lax.psum(contract_first(matches, owned_grads.reshape(-1, feature)), "dp")
    new_table = row_table - STEP_SIZE * row_sums
    return (in_grad[None], out_grad[None], gate_grad[None], tower_grad, new_table)


def solution(mesh):
    in_specs = (
        P(("expert", "dp"), None),
        P(("expert", "dp"), None),
        P(("expert", "dp"), None),
        P("expert", None, None),
        P("expert", None, None),
        P(),
        P(),
        P(),
        P(("expert", "dp")),
        P(("expert", "dp")),
        P(("expert", "dp")),
        P("expert", None),
    )
    out_specs = (
        P("expert", "dp", None),
        P("expert", "dp", None),
        P("expert", None, None),
        P(),
        P("expert", None),
    )
    return jax.shard_map(
        on_device, mesh=mesh, in_specs=in_specs, out_specs=out_specs, check_vma=False
    )
```

time: 218 us -> 192 us (0.88)
  local copies, waits for them, and re-layouts: 40.9 us -> 18.3 us
  matrix products: 42.1 us -> 38.4 us
  blocking collectives: 39.3 us -> 43 us
  starting transfers between devices: 30.2 us -> 26.6 us
    dot_general x3 -> x2, matrix products: 16.3 us -> 6.63 us  [contract_last(): lax.dot_general(left, right, (((1,), (1,)), ((), ())), preferred_element_...]
    dot_general x6 -> x11, matrix products: 8.68 us -> 17.6 us  [the longest x1 4.52 us: on_device(): hidden_sum = jnp.dot(coefs, hidden_f32, precision=lax.Precision.HIGH)]
    convert_element_type x2 -> x5, other arithmetic: 0.85 us -> 8.94 us  [the longest x1 8.09 us: on_device(): pre_grad = (hidden_grad * silu_grad(pre_silu)).astype(jnp.bfloat16)]
    scatter x2 -> x0, local copies, waits for them, and re-layouts: 6.12 us -> none  [the longest x1 3.06 us: on_device(): jnp.zeros((owner_count * capacity, feature), jnp.bfloat16).at[slot_index]]
    broadcast_in_dim x2 -> x0, local copies, waits for them, and re-layouts: 5.78 us -> none  [the longest x1 4.73 us: on_device(): out_grad = summed[:, feature:][None]]
    unnamed x57 -> x27, local copies, waits for them, and re-layouts: 14.4 us -> 9.99 us
    gather x3 -> x0, local copies, waits for them, and re-layouts: 4 us -> none  [the longest x2 2.06 us: on_device(): returned.reshape(-1, feature)[slot_index].astype(jnp.float32)]
    concatenate x1 -> x0, other arithmetic: 3.77 us -> none  [on_device(): jnp.concatenate([contract_first(pre_grad, inputs), contract_first(hidden_...]
  transfers between devices with their start and end apart: 8 -> 9, of which waited for: 5 -> 6; matrix products, arithmetic and copies ran while one was open for 20% -> 19% of each run, Pallas kernels for 0% -> 0%
where the time goes in v1:
time: 192 us; the launch traced here: 191 us
  blocking collectives  43 us (22%)
  matrix products  38.4 us (20%)
  waiting for transfers between devices  35.3 us (18%)
  starting transfers between devices  26.6 us (14%)
  local copies, waits for them, and re-layouts  18.3 us (10%)
  other arithmetic  15.6 us (8%)
  between operations  14 us (7%)
    psum x1, blocking collectives, on_device(): tower_grad = lax.psum(tower_local, ('expert', 'dp'))  40 us
    all_to_all x6, waiting for transfers between devices, swap(): lax.all_to_all(values, 'expert', split_axis=0, concat_axis=0, tiled=True)  35.3 us
    all_to_all x6, starting transfers between devices, swap(): lax.all_to_all(values, 'expert', split_axis=0, concat_axis=0, tiled=True)  26.4 us
    dot_general x3, matrix products, contract_first(): lax.dot_general(left, right, (((0,), (0,)), ((), ())), preferred_element_...  10.6 us
    unnamed x27, local copies, waits for them, and re-layouts  9.99 us
    convert_element_type x1, other arithmetic, on_device(): pre_grad = (hidden_grad * silu_grad(pre_silu)).astype(jnp.bfloat16)  8.09 us
    dot_general x2, matrix products, contract_last(): lax.dot_general(left, right, (((1,), (1,)), ((), ())), preferred_element_...  6.63 us
    dot_general x1, matrix products, on_device(): hidden_sum = jnp.dot(coefs, hidden_f32, precision=lax.Precision.HIGH)  4.52 us
  transfers between devices with their start and end apart: 9, of which 6 were waited for; matrix products, arithmetic and copies ran while one was open for 19% of the time, Pallas kernels for 0%

profile of v1, /device:TPU:0, one launch (start us, length us, event | category | flops | bytes accessed | tf_op | source)
XLA Modules:
  0.0 191.2 jit_solution(2236055928645693339)
XLA Ops:
  7.2 0.8 fusion.69
  8.0 0.1 fusion.48
  8.2 0.2 fusion.30
  8.4 0.1 fusion.43
  8.5 0.8 multiply_add_fusion.2
  9.3 2.1 %convolution_convert_fusion = bf16[768,256]{1,0:T(8,128)(2,1)} fusion(bf16[256,256]{1,0:T(8,128)(2,1)} %param.12, s32[256]{0:T(256)S(1)} %bitcast.97, s32[256]{0:T(256)S(1)} %bitcast.93), kind=kOutput, calls=%fused_computation.15 | convolution fusion | flops 102432768 | bytes 526336 | tf_op jit(solution)/shard_map/dot_general | solution.py:17
  11.4 8.3 %all-to-all-start = ((bf16[16,48,256]{2,1,0:T(8,128)(2,1)}), bf16[16,48,256]{2,1,0:T(8,128)(2,1)S(1)}, u32[]{:S(2)}, u32[]{:S(2)}) async-start(bf16[16,48,256]{2,1,0:T(8,128)(2,1)} %bitcast.8), calls=%async_computation | async-start | bytes 786432 | tf_op jit(solution)/shard_map/all_to_all | solution.py:63
  19.8 3.3 %fusion.6 = f32[2,4096]{1,0:T(2,128)S(1)} fusion(f32[2,256]{1,0:T(2,128)} %param.18, bf16[1,4096,256]{2,1,0:T(8,128)(2,1)} %param.16), kind=kOutput, calls=%fused_computation.10 | convolution fusion | flops 25165824 | bytes 2131968 | tf_op jit(solution)/shard_map/dot_general | solution.py:67
  23.1 9.3 %all-to-all-done = bf16[16,48,256]{2,1,0:T(8,128)(2,1)S(1)} async-done(((bf16[16,48,256]{2,1,0:T(8,128)(2,1)}), bf16[16,48,256]{2,1,0:T(8,128)(2,1)S(1)}, u32[]{:S(2)}, u32[]{:S(2)}) %all-to-all-start) | async-done | bytes 393248 | tf_op jit(solution)/shard_map/all_to_all | solution.py:63
  32.4 6.4 %multiply_convert_fusion.1 = (bf16[768,4096]{1,0:T(8,128)(2,1)S(1)}, f32[768,4096]{1,0:T(8,128)}) fusion(bf16[768,256]{1,0:T(8,128)(2,1)S(1)} %bitcast.70, bf16[1,4096,256]{2,1,0:T(8,128)(2,1)S(1)} %copy-done), kind=kOutput, calls=%fused_computation.2 | convolution fusion | flops 1626341376 | bytes 21364736 | tf_op jit(solution)/shard_map/dot_general | solution.py:23
  38.8 2.6 %copy-done.1 = bf16[768,4096]{1,0:T(8,128)(2,1)} copy-done((bf16[768,4096]{1,0:T(8,128)(2,1)}, bf16[768,4096]{1,0:T(8,128)(2,1)S(1)}, u32[]{:S(2)}) %copy-start.1) | copy-done | bytes 6291480
  41.4 3.3 %fusion.70 = f32[2,768]{1,0:T(2,128)S(1)} fusion(f32[2,4096]{1,0:T(2,128)S(1)} %fusion.6, bf16[768,4096]{1,0:T(8,128)(2,1)S(1)} %get-tuple-element.26), kind=kOutput, calls=%fused_computation.99 | convolution fusion | flops 37748736 | bytes 6330368 | tf_op jit(solution)/shard_map/dot_general | solution.py:73
  44.7 0.1 reshape.237
  44.8 0.6 copy.46
  45.5 3.6 %all-to-all-start.1 = ((f32[16,2,48]{2,1,0:T(2,128)}), f32[16,2,48]{2,1,0:T(2,128)S(1)}, u32[]{:S(2)}, u32[]{:S(2)}) async-start(f32[16,2,48]{2,1,0:T(2,128)} %bitcast.66), calls=%async_computation.1 | async-start | bytes 32768 | tf_op jit(solution)/shard_map/all_to_all | solution.py:63
  49.1 0.2 fusion.12
  49.3 7.1 %all-to-all-done.1 = f32[16,2,48]{2,1,0:T(2,128)S(1)} async-done(((f32[16,2,48]{2,1,0:T(2,128)}), f32[16,2,48]{2,1,0:T(2,128)S(1)}, u32[]{:S(2)}, u32[]{:S(2)}) %all-to-all-start.1) | async-done | bytes 6176 | tf_op jit(solution)/shard_map/all_to_all | solution.py:63
  56.4 0.1 reshape.238
  56.5 0.5 fusion.17
  57.0 0.1 copy-done.10
  57.0 0.6 subtract_multiply_fusion
  57.6 0.4 fusion.16
  58.0 0.4 convolution_add_fusion.1
  58.5 0.1 reshape.239
  58.6 0.7 reshape.278
  59.3 3.5 %all-to-all-start.2 = ((f32[16,1,192]{2,1,0:T(1,128)}), f32[16,1,192]{2,1,0:T(1,128)S(1)}, u32[]{:S(2)}, u32[]{:S(2)}) async-start(f32[16,1,192]{2,1,0:T(1,128)} %reshape.278), calls=%async_computation.2 | async-start | bytes 32768 | tf_op jit(solution)/shard_map/all_to_all | solution.py:63
  62.8 7.3 %all-to-all-done.2 = f32[16,1,192]{2,1,0:T(1,128)S(1)} async-done(((f32[16,1,192]{2,1,0:T(1,128)}), f32[16,1,192]{2,1,0:T(1,128)S(1)}, u32[]{:S(2)}, u32[]{:S(2)}) %all-to-all-start.2) | async-done | bytes 12320 | tf_op jit(solution)/shard_map/all_to_all | solution.py:63
  70.1 0.5 broadcast.154
  70.6 0.7 reduce.12
  71.3 0.1 reshape.279
  71.4 0.1 mul.184
  71.5 0.1 mul.189
  71.6 8.1 %multiply_convert_fusion = bf16[768,4096]{1,0:T(8,128)(2,1)S(1)} fusion(f32[768,4096]{1,0:T(8,128)} %get-tuple-element.27, f32[4096]{0:T(1024)S(1)} %bitcast.81, f32[768]{0:T(1024)S(1)} %mul.189, f32[4096]{0:T(1024)S(1)} %bitcast.80, f32[768]{0:T(1024)S(1)} %mul.184), kind=kLoop, calls=%fused_computation.1 | loop fusion | flops 37748736 | bytes 18913280 | tf_op jit(solution)/shard_map/convert_element_type | solution.py:100
  79.7 2.6 %copy-done.2 = bf16[768,4096]{1,0:T(8,128)(2,1)} copy-done((bf16[768,4096]{1,0:T(8,128)(2,1)}, bf16[768,4096]{1,0:T(8,128)(2,1)S(1)}, u32[]{:S(2)}) %copy-start.2) | copy-done | bytes 6291480
  82.3 2.5 %fusion.9 = bf16[768,256]{1,0:T(8,128)(2,1)} fusion(bf16[768,4096]{1,0:T(8,128)(2,1)S(1)} %multiply_convert_fusion, bf16[1,4096,256]{2,1,0:T(8,128)(2,1)S(1)} %copy-done), kind=kOutput, calls=%fused_computation.16 | convolution fusion | flops 1610809344 | bytes 8781824 | tf_op jit(solution)/shard_map/dot_general | solution.py:101
  84.9 3.7 %all-to-all-start.4 = ((bf16[16,48,256]{2,1,0:T(8,128)(2,1)}), bf16[16,48,256]{2,1,0:T(8,128)(2,1)S(1)}, u32[]{:S(2)}, u32[]{:S(2)}) async-start(bf16[16,48,256]{2,1,0:T(8,128)(2,1)} %bitcast.73), calls=%async_computation.5 | async-start | bytes 786432 | tf_op jit(solution)/shard_map/all_to_all | solution.py:63
  88.6 0.7 all_to_all.24
  89.3 0.1 mul.205
  89.4 1.0 convolution_bitcast_fusion
  90.4 7.6 %all-to-all-done.4 = bf16[16,48,256]{2,1,0:T(8,128)(2,1)S(1)} async-done(((bf16[16,48,256]{2,1,0:T(8,128)(2,1)}), bf16[16,48,256]{2,1,0:T(8,128)(2,1)S(1)}, u32[]{:S(2)}, u32[]{:S(2)}) %all-to-all-start.4) | async-done | bytes 393248 | tf_op jit(solution)/shard_map/all_to_all | solution.py:63
  98.0 3.7 %all-to-all-start.3 = ((s32[16,1,32]{2,1,0:T(1,128)}), s32[16,1,32]{2,1,0:T(1,128)S(1)}, u32[]{:S(2)}, u32[]{:S(2)}) async-start(s32[16,1,32]{2,1,0:T(1,128)} %all_to_all.24), calls=%async_computation.4 | async-start | bytes 16384 | tf_op jit(solution)/shard_map/all_to_all | solution.py:63
  101.8 1.3 convolution_add_fusion
  103.1 1.6 gather_fusion
  104.7 0.8 multiply_convert_fusion.2
  105.5 3.5 %all-to-all-done.3 = s32[16,1,32]{2,1,0:T(1,128)S(1)} async-done(((s32[16,1,32]{2,1,0:T(1,128)}), s32[16,1,32]{2,1,0:T(1,128)S(1)}, u32[]{:S(2)}, u32[]{:S(2)}) %all-to-all-start.3) | async-done | bytes 2080 | tf_op jit(solution)/shard_map/all_to_all | solution.py:63
  109.0 3.5 %all-to-all-start.5 = ((bf16[16,32,256]{2,1,0:T(8,128)(2,1)}), bf16[16,32,256]{2,1,0:T(8,128)(2,1)S(1)}, u32[]{:S(2)}, u32[]{:S(2)}) async-start(bf16[16,32,256]{2,1,0:T(8,128)(2,1)} %multiply_convert_fusion.2), calls=%async_computation.6 | async-start | bytes 524288 | tf_op jit(solution)/shard_map/all_to_all | solution.py:63
  112.6 0.5 broadcast.150
  113.1 0.7 reduce.11
  113.8 0.1 eq.93
  113.9 0.1 slice.71
  114.0 4.5 %fusion.72 = f32[2,4096]{1,0:T(2,128)S(1)} fusion(f32[2,768]{1,0:T(2,128)S(1)} %slice.71, bf16[768,4096]{1,0:T(8,128)(2,1)} %copy-done.1), kind=kOutput, calls=%fused_computation.101 | convolution fusion | flops 37748736 | bytes 6330368 | tf_op jit(solution)/shard_map/dot_general | solution.py:112
  118.5 2.0 %copy.35 = f32[2,4096]{0,1:T(8,128)} copy(f32[2,4096]{1,0:T(2,128)S(1)} %fusion.72) | data formatting | bytes 65536
  120.5 0.5 all-to-all-done.5
  121.0 1.8 fusion.8
  122.9 6.6 %fusion.71 = f32[4096,256]{1,0:T(8,128)} fusion(bf16[768,4096]{1,0:T(8,128)(2,1)} %copy-done.2, bf16[768,256]{1,0:T(8,128)(2,1)S(1)} %bitcast.71), kind=kOutput, calls=%fused_computation.100 | convolution fusion | flops 1610612736 | bytes 10878976 | tf_op jit(solution)/shard_map/dot_general | solution.py:17
  129.6 2.7 %fusion.4 = f32[2,256]{1,0:T(2,128)S(1)} fusion(f32[2,4096]{1,0:T(2,128)S(1)} %fusion.72, bf16[1,4096,256]{2,1,0:T(8,128)(2,1)} %param.16), kind=kOutput, calls=%fused_computation.8 | convolution fusion | flops 25165824 | bytes 2131968 | tf_op jit(solution)/shard_map/dot_general | solution.py:117
  132.3 40.0 %psum.22 = f32[2,256]{1,0:T(2,128)} all-reduce(f32[2,256]{1,0:T(2,128)S(1)} %fusion.4), channel_id=1, replica_groups=mesh['expert'=16,'dp'=2] {'expert','dp'}, use_global_device_ids=true, to_apply=%region_7.8 | all-reduce | flops 512 | bytes 4096 | tf_op jit(solution)/shard_map/psum | solution.py:118
  172.3 0.4 convolution_bitcast_fusion.1
  172.6 3.0 %psum.21 = f32[1,2,256]{2,1,0:T(2,128)} all-reduce(f32[1,2,256]{2,1,0:T(2,128)S(1)} %convolution_bitcast_fusion.1), channel_id=1, replica_groups=mesh['expert'=16,'dp'=2] {'dp'}, use_global_device_ids=true, to_apply=%region_6.7 | all-reduce | flops 512 | bytes 4096 | tf_op jit(solution)/shard_map/psum | solution.py:119
  175.7 2.8 %fusion.66 = (f32[1,2048]{0,1:T(8,128)}, f32[1,2048]{0,1:T(8,128)S(1)}) fusion(f32[2,2048]{0,1:T(8,128)} %bitcast.68), kind=kLoop, calls=%fused_computation.95 | loop fusion | bytes 32768 | tf_op jit(solution)/shard_map/slice | solution.py:121
  178.5 1.6 copy.37
  180.0 0.3 copy.38
  180.4 1.7 multiply_add_fusion
  182.0 2.6 %multiply_subtract_fusion = f32[1024,256]{1,0:T(8,128)} fusion(f32[1024,256]{1,0:T(8,128)} %param.23, f32[1024,256]{1,0:T(8,128)} %all-reduce.2.cloned.1.call-done), kind=kLoop, calls=%fused_computation.23 | loop fusion | flops 524288 | bytes 3145728 | tf_op jit(solution)/shard_map/sub | solution.py:127
  (42 shorter events, 0.4 us)
Async XLA Ops:
  7.2 25.2 %copy-start = (bf16[1,4096,256]{2,1,0:T(8,128)(2,1)S(1)}, bf16[1,4096,256]{2,1,0:T(8,128)(2,1)}, u32[]{:S(2)}) copy-start(bf16[1,4096,256]{2,1,0:T(8,128)(2,1)} %param.15) | copy-start | bytes 6291460
  11.4 21.0 %all-to-all-start = ((bf16[16,48,256]{2,1,0:T(8,128)(2,1)}), bf16[16,48,256]{2,1,0:T(8,128)(2,1)S(1)}, u32[]{:S(2)}, u32[]{:S(2)}) async-start(bf16[16,48,256]{2,1,0:T(8,128)(2,1)} %bitcast.8), calls=%async_computation | async-start | bytes 786432 | tf_op jit(solution)/shard_map/all_to_all | solution.py:63
  38.8 2.6 %copy-start.1 = (bf16[768,4096]{1,0:T(8,128)(2,1)}, bf16[768,4096]{1,0:T(8,128)(2,1)S(1)}, u32[]{:S(2)}) copy-start(bf16[768,4096]{1,0:T(8,128)(2,1)S(1)} %get-tuple-element.26) | copy-start | bytes 18874372
  38.8 10.2 %copy-start.3 = (bf16[256,256]{1,0:T(8,128)(2,1)S(1)}, bf16[256,256]{1,0:T(8,128)(2,1)}, u32[]{:S(2)}) copy-start(bf16[256,256]{1,0:T(8,128)(2,1)} %param.12) | copy-start | bytes 393220
  38.8 10.3 %copy-start.4 = (bf16[16,2,256]{2,1,0:T(2,128)(2,1)S(1)}, bf16[16,2,256]{2,1,0:T(2,128)(2,1)}, u32[]{:S(2)}) copy-start(bf16[16,2,256]{2,1,0:T(2,128)(2,1)} %param.17) | copy-start | bytes 49156
  38.8 18.1 %copy-start.9 = (s32[256,2]{0,1:T(2,128)S(1)}, s32[256,2]{0,1:T(2,128)}, u32[]{:S(2)}) copy-start(s32[256,2]{0,1:T(2,128)} %param.14) | copy-start | bytes 6148
  38.8 18.2 %copy-start.10 = (f32[2]{0:T(128)S(1)}, f32[2]{0:T(128)}, u32[]{:S(2)}) copy-start(f32[2]{0:T(128)} %param.19) | copy-start | bytes 28
  45.5 10.9 %all-to-all-start.1 = ((f32[16,2,48]{2,1,0:T(2,128)}), f32[16,2,48]{2,1,0:T(2,128)S(1)}, u32[]{:S(2)}, u32[]{:S(2)}) async-start(f32[16,2,48]{2,1,0:T(2,128)} %bitcast.66), calls=%async_computation.1 | async-start | bytes 32768 | tf_op jit(solution)/shard_map/all_to_all | solution.py:63
  59.3 10.8 %all-to-all-start.2 = ((f32[16,1,192]{2,1,0:T(1,128)}), f32[16,1,192]{2,1,0:T(1,128)S(1)}, u32[]{:S(2)}, u32[]{:S(2)}) async-start(f32[16,1,192]{2,1,0:T(1,128)} %reshape.278), calls=%async_computation.2 | async-start | bytes 32768 | tf_op jit(solution)/shard_map/all_to_all | solution.py:63
  79.7 2.7 %copy-start.2 = (bf16[768,4096]{1,0:T(8,128)(2,1)}, bf16[768,4096]{1,0:T(8,128)(2,1)S(1)}, u32[]{:S(2)}) copy-start(bf16[768,4096]{1,0:T(8,128)(2,1)S(1)} %multiply_convert_fusion) | copy-start | bytes 18874372
  82.3 6.3 %copy-start.6 = (s32[512]{0:T(512)S(1)}, s32[512]{0:T(512)}, u32[]{:S(2)}) copy-start(s32[512]{0:T(512)} %param.20) | copy-start | bytes 6148
  82.3 7.0 %copy-start.7 = (f32[512]{0:T(512)S(1)}, f32[512]{0:T(512)}, u32[]{:S(2)}) copy-start(f32[512]{0:T(512)} %param.22) | copy-start | bytes 6148
  82.3 7.1 %copy-start.8 = (s32[512]{0:T(512)S(1)}, s32[512]{0:T(512)}, u32[]{:S(2)}) copy-start(s32[512]{0:T(512)} %param.21) | copy-start | bytes 6148
  84.9 13.2 %all-to-all-start.4 = ((bf16[16,48,256]{2,1,0:T(8,128)(2,1)}), bf16[16,48,256]{2,1,0:T(8,128)(2,1)S(1)}, u32[]{:S(2)}, u32[]{:S(2)}) async-start(bf16[16,48,256]{2,1,0:T(8,128)(2,1)} %bitcast.73), calls=%async_computation.5 | async-start | bytes 786432 | tf_op jit(solution)/shard_map/all_to_all | solution.py:63
  98.0 11.0 %all-to-all-start.3 = ((s32[16,1,32]{2,1,0:T(1,128)}), s32[16,1,32]{2,1,0:T(1,128)S(1)}, u32[]{:S(2)}, u32[]{:S(2)}) async-start(s32[16,1,32]{2,1,0:T(1,128)} %all_to_all.24), calls=%async_computation.4 | async-start | bytes 16384 | tf_op jit(solution)/shard_map/all_to_all | solution.py:63
  109.0 12.0 %all-to-all-start.5 = ((bf16[16,32,256]{2,1,0:T(8,128)(2,1)}), bf16[16,32,256]{2,1,0:T(8,128)(2,1)S(1)}, u32[]{:S(2)}, u32[]{:S(2)}) async-start(bf16[16,32,256]{2,1,0:T(8,128)(2,1)} %multiply_convert_fusion.2), calls=%async_computation.6 | async-start | bytes 524288 | tf_op jit(solution)/shard_map/all_to_all | solution.py:63
  112.5 63.1 %reduce-scatter.7.cloned.1.call-start = ((), (), s32[]{:S(2)}) async-start(), calls=%async_computation.10 | async-start | bytes 3145728
  120.5 61.6 %all-reduce.2.cloned.1.call-start = ((), (), s32[]{:S(2)}) async-start(), calls=%async_computation.9 | async-start | bytes 2097152 | tf_op jit(solution)/shard_map/psum | solution.py:126
  122.9 6.7 %copy-start.5 = (f32[2,256]{1,0:T(2,128)S(1)}, f32[2,256]{1,0:T(2,128)}, u32[]{:S(2)}) copy-start(f32[2,256]{1,0:T(2,128)} %param.18) | copy-start | bytes 6148
  122.9 61.8 %reduce-scatter.5.cloned.1.call-start = ((), (), s32[]{:S(2)}) async-start(), calls=%async_computation.8 | async-start | bytes 6291456 | tf_op jit(solution)/shard_map/reduce_scatter | solution.py:113
Sparse Core Ops, SparseCore 0:
  120.6 10.9 reduce-scatter.6
  134.0 20.6 all-reduce.1
  157.6 13.2 reduce-scatter.4

commit v2 on v1

v2 whole, which is shorter than its diff:
```python
import functools

import jax
import jax.numpy as jnp
from jax import lax
from jax.experimental import pallas as pl
from jax.experimental.pallas import tpu as pltpu
from jax.sharding import PartitionSpec as P

LOSS_SCALE = 32.0
STEP_SIZE = 0.25
F32, BF16 = jnp.float32, jnp.bfloat16
MESH = pl.DeviceIdType.MESH
VMEM_LIMIT = 62 * 2**20


def mm(left, right, left_dim=1, right_dim=0):
    return lax.dot_general(
        left, right, (((left_dim,), (right_dim,)), ((), ())), preferred_element_type=F32
    )


def nt(left, right):
    return mm(left, right, 1, 1)


def halves(value):
    high = value.astype(BF16).astype(F32)
    return high, value - high


def stacked(value):
    return jnp.concatenate(halves(value), axis=0).astype(BF16)


def folded(value):
    return value[:8] + value[8:]


def sigmoid(value):
    return 0.5 * jnp.tanh(0.5 * value) + 0.5


def iota(shape, dim):
    return lax.broadcasted_iota(jnp.int32, shape, dim)


def one_hot(condition):
    return jnp.where(condition, 1.0, 0.0)


def exchange(count, me, source, target, send_sem, recv_sem):
    def copy(peer, slot):
        return pltpu.make_async_remote_copy(
            src_ref=source.at[peer],
            dst_ref=target.at[slot],
            send_sem=send_sem.at[peer],
            recv_sem=recv_sem.at[slot],
            device_id={"expert": peer},
            device_id_type=MESH,
        )

    def start():
        @pl.loop(1, count)
        def _(step):
            copy(lax.rem(me + step, count), me).start()

        target[me] = source[me]

    def wait():
        @pl.loop(1, count)
        def _(step):
            peer = lax.rem(me + step, count)
            copy(peer, peer).wait_recv()

    def drain():
        @pl.loop(1, count)
        def _(step):
            copy(lax.rem(me + step, count), me).wait_send()

    return start, wait, drain


def kernel(
    sizes,
    pooled_ref,
    routes_ref,
    routes_rows_ref,
    labels_ref,
    in_hbm,
    out_hbm,
    gate_ref,
    tower_ref,
    bias_ref,
    bag_rows_ref,
    bag_sample_ref,
    bag_weight_ref,
    in_parts_ref,
    hidden_parts_ref,
    small_ref,
    grads_ref,
    rows_ref,
    in_ref,
    out_ref,
    turned_ref,
    proj_rows_ref,
    proj_cols_ref,
    act_ref,
    slope_ref,
    pre_ref,
    place_ref,
    a_send,
    a_recv,
    b_send,
    b_recv,
    c_send,
    c_recv,
    d_send,
    d_recv,
    e_send,
    e_recv,
    r_recv,
    t_send,
    t_recv,
    s_send,
    s_recv,
    in_other,
    hidden_other,
    rows_acc,
    back_acc,
    send_sem,
    recv_sem,
    dp_send,
    dp_recv,
    local_sem,
):
    count, cap, chunk, chunks = sizes
    rows_all = count * cap
    tok_rows = pooled_ref.shape[0]
    me, core = lax.axis_index("expert"), lax.axis_index("dp")
    other = 1 - core
    half = chunks // 2

    def phase(index, source, target):
        return exchange(count, me, source, target, send_sem.at[index], recv_sem.at[index])

    a_start, a_wait, a_drain = phase(0, a_send, a_recv)
    b_start, b_wait, b_drain = phase(1, b_send, b_recv)
    c_start, c_wait, c_drain = phase(2, c_send, c_recv)
    d_start, d_wait, d_drain = phase(3, d_send, d_recv)
    e_start, e_wait, e_drain = phase(4, e_send, e_recv)
    r_start, r_wait, r_drain = phase(5, bag_rows_ref, r_recv)
    t_start, t_wait, t_drain = phase(6, t_send, t_recv)

    def to_other(index, source, target):
        return pltpu.make_async_remote_copy(
            src_ref=source,
            dst_ref=target,
            send_sem=dp_send.at[index],
            recv_sem=dp_recv.at[index],
            device_id={"dp": other},
            device_id_type=MESH,
        )

    barrier = pltpu.get_barrier_semaphore()

    @pl.loop(1, count)
    def _(step):
        pl.semaphore_signal(
            barrier, inc=1, device_id={"expert": lax.rem(me + step, count)}, device_id_type=MESH
        )

    pl.semaphore_signal(barrier, inc=1, device_id={"dp": other}, device_id_type=MESH)
    load_out = pltpu.make_async_copy(out_hbm, out_ref, local_sem.at[0])
    load_in = pltpu.make_async_copy(in_hbm, in_ref, local_sem.at[1])
    load_out.start()
    load_in.start()

    first_row, second_row = routes_rows_ref[0:1, :], routes_rows_ref[1:2, :]
    first_map = one_hot(iota((count, tok_rows), 0) == first_row)
    second_map = one_hot(iota((count, tok_rows), 0) == second_row)
    above = one_hot(
        iota((tok_rows, tok_rows), 0) < iota((tok_rows, tok_rows), 1)
    ).astype(BF16)
    first_total = jnp.sum(first_map, axis=1, keepdims=True)
    first_rank = jnp.sum(first_map * mm(first_map.astype(BF16), above), axis=0, keepdims=True)
    second_rank = jnp.sum(
        second_map * (mm(second_map.astype(BF16), above) + first_total), axis=0, keepdims=True
    )
    first_slot = first_rank.astype(jnp.int32) + first_row * cap
    second_slot = second_rank.astype(jnp.int32) + second_row * cap
    places = iota((rows_all, tok_rows), 0)
    fill = one_hot((places == first_slot) | (places == second_slot)).astype(BF16)
    place_ref[...] = fill
    a_send[...] = mm(fill, pooled_ref[...]).astype(BF16).reshape(a_send.shape)
    pl.semaphore_wait(barrier, count)
    a_start()
    r_start()

    lanes = iota((128, tok_rows), 0)
    first_at = one_hot(lanes == first_rank.astype(jnp.int32)).astype(BF16)
    second_at = one_hot(lanes == second_rank.astype(jnp.int32)).astype(BF16)
    signed = first_map - second_map
    row_of = iota((8, tok_rows), 0)
    gate_logit = jnp.zeros((8, tok_rows), F32)
    for task in range(2):
        logits = nt(gate_ref[task], pooled_ref[...])
        gate_logit = jnp.where(
            row_of == task, jnp.sum(signed * logits, axis=0, keepdims=True), gate_logit
        )
    gate_first = sigmoid(gate_logit)
    gate_second = 1.0 - gate_first
    tower_high, tower_low = halves(tower_ref[...])
    tower_high, tower_low = tower_high.astype(BF16), tower_low.astype(BF16)
    load_out.wait()
    load_in.wait()

    @pl.loop(0, chunks)
    def _(step):
        span = pl.ds(pl.multiple_of(step * chunk, chunk), chunk)
        weights = out_ref[span, :]
        proj_rows_ref[step] = stacked(nt(tower_high, weights) + nt(tower_low, weights))
        proj_cols_ref[span, :] = nt(weights, tower_high) + nt(weights, tower_low)
        turned_ref[step] = in_ref[span, :].T

    a_wait()
    rows_acc[...] = jnp.zeros_like(rows_acc)

    @pl.loop(0, chunks)
    def _(step):
        span = pl.ds(pl.multiple_of(step * chunk, chunk), chunk)
        before = nt(in_ref[span, :], a_recv[...].reshape(rows_all, -1))
        sigma = sigmoid(before)
        act = before * sigma
        slope_ref[span, :] = (sigma + act * (1.0 - sigma)).astype(slope_ref.dtype)
        act = act.astype(BF16)
        act_ref[span, :] = act
        rows_acc[...] += mm(proj_rows_ref[step], act)

    dots = folded(rows_acc[...])

    @pl.loop(0, count)
    def _(peer):
        b_send[peer] = pltpu.roll(dots, lax.rem(rows_all - peer * cap, rows_all), 1)[:, :128]

    b_start()
    b_wait()
    owner_of = iota((count * 8, tok_rows), 0) // 8
    first_mask = one_hot(owner_of == first_row)
    second_mask = one_hot(owner_of == second_row)
    got_high, got_low = halves(
        jnp.where(iota((count * 8, 128), 1) < cap, b_recv[...].reshape(count * 8, 128), 0.0)
    )

    def pick(mask, where):
        found = mm(got_high.astype(BF16), where) + mm(got_low.astype(BF16), where)
        return jnp.sum((mask * found).reshape(count, 8, tok_rows), axis=0)

    first_dot, second_dot = pick(first_mask, first_at), pick(second_mask, second_at)
    task_logit = gate_first * first_dot + gate_second * second_dot + bias_ref[...]
    logit_grad = LOSS_SCALE * (sigmoid(task_logit) - labels_ref[...])
    first_grad = logit_grad * (first_dot - second_dot) * gate_first * gate_second
    lower = pltpu.roll(first_grad, 2, 0)
    keep = row_of < 4
    first_vals = jnp.where(keep, jnp.where(row_of < 2, gate_first * logit_grad, lower), 0.0)
    second_vals = jnp.where(keep, jnp.where(row_of < 2, gate_second * logit_grad, -lower), 0.0)

    def spread(vals, mask, where):
        wide = jnp.broadcast_to(vals[None], (count, 8, tok_rows)).reshape(count * 8, tok_rows)
        high, low = halves(wide * mask)
        return nt(high.astype(BF16), where) + nt(low.astype(BF16), where)

    c_send[...] = (
        spread(first_vals, first_mask, first_at) + spread(second_vals, second_mask, second_at)
    ).reshape(c_send.shape)
    c_start()
    gate_input = jnp.zeros((tok_rows, pooled_ref.shape[1]), F32)
    for task in range(2):
        high, low = halves(signed * first_grad[task : task + 1, :])
        weights = gate_ref[task]
        gate_input += mm(high.astype(BF16), weights, 0, 0) + mm(low.astype(BF16), weights, 0, 0)
    c_wait()
    coefs = jnp.zeros((8, rows_all), F32)
    blank = jnp.zeros((8, rows_all - 128), F32)

    def place(peer, total):
        return total + pltpu.roll(
            jnp.concatenate([c_recv[peer], blank], axis=1), peer * cap, 1
        )

    coefs = lax.fori_loop(0, count, place, coefs)
    coef_zero, coef_one = coefs[0:1, :], coefs[1:2, :]
    back_acc[...] = jnp.zeros_like(back_acc)

    @pl.loop(0, chunks)
    def _(step):
        span = pl.ds(pl.multiple_of(step * chunk, chunk), chunk)
        cols = proj_cols_ref[span, :]
        hidden_grad = cols[:, 0:1] * coef_zero + cols[:, 1:2] * coef_one
        grad = (hidden_grad * slope_ref[span, :].astype(F32)).astype(BF16)
        pre_ref[span, :] = grad
        back_acc[...] += mm(turned_ref[step], grad)

    d_send[...] = back_acc[...].T.astype(BF16).reshape(d_send.shape)
    d_start()

    coef_rows = stacked(coefs)

    def weight_chunk(step, in_target, hidden_target, slot):
        span = pl.ds(pl.multiple_of(step * chunk, chunk), chunk)
        in_target[pl.ds(pl.multiple_of(slot * chunk, chunk), chunk), :] = mm(
            pre_ref[span, :], a_recv[...].reshape(rows_all, -1)
        )
        hidden = folded(nt(coef_rows, act_ref[span, :]))
        hidden_target[slot] = hidden
        return folded(mm(stacked(hidden), out_ref[span, :]))

    tower = jnp.zeros((8, pooled_ref.shape[1]), F32)
    tower = lax.fori_loop(
        0,
        half,
        lambda i, total: total + weight_chunk(other * half + i, in_other, hidden_other, i),
        tower,
    )
    in_copy = to_other(0, in_other, in_parts_ref.at[1])
    hidden_copy = to_other(1, hidden_other, hidden_parts_ref.at[1])
    in_copy.start()
    hidden_copy.start()
    d_wait()
    pooled_grad = gate_input + mm(
        place_ref[...], d_recv[...].reshape(rows_all, -1), 0, 0
    )
    bag = one_hot(iota((bag_sample_ref.shape[0], tok_rows), 1) == bag_sample_ref[...]).astype(BF16)
    high, low = halves(pooled_grad)
    bag_grad = mm(bag, high.astype(BF16)) + mm(bag, low.astype(BF16))
    e_send[...] = (bag_weight_ref[...] * bag_grad).astype(BF16).reshape(e_send.shape)
    e_start()
    tower = lax.fori_loop(
        0,
        half,
        lambda i, total: total
        + weight_chunk(core * half + i, in_parts_ref.at[0], hidden_parts_ref.at[0], i),
        tower,
    )
    gate = folded(mm(coef_rows, a_recv[...].reshape(rows_all, -1)))
    tile = jnp.where(iota(tower.shape, 0) < 2, tower, gate)
    t_send[...] = jnp.broadcast_to(tile[None], t_send.shape)
    t_start()
    r_wait()
    e_wait()
    grads_copy = to_other(2, e_recv, grads_ref.at[core])
    rows_copy = to_other(3, r_recv, rows_ref.at[core])
    grads_copy.start()
    rows_copy.start()
    grads_ref[core] = e_recv[...]
    rows_ref[core] = r_recv[...]
    t_wait()
    summed = lax.fori_loop(0, count, lambda i, total: total + t_recv[i], jnp.zeros_like(tower))
    mine = jnp.where(iota(tower.shape, 0) < 2, summed, tile)
    s_send[...] = mine
    small_copy = to_other(4, s_send, s_recv)
    small_copy.start()
    small_copy.wait()
    small_ref[...] = mine + s_recv[...]
    for copy in (in_copy, hidden_copy, grads_copy, rows_copy):
        copy.wait()
    for drain in (a_drain, b_drain, c_drain, d_drain, e_drain, r_drain, t_drain):
        drain()


def on_device(
    pooled,
    routes,
    labels,
    in_weight,
    out_weight,
    gate_weight,
    tower_weight,
    tower_bias,
    bag_rows,
    bag_sample,
    bag_weight,
    row_table,
):
    count = lax.axis_size("expert")
    tok_rows, feature = pooled.shape
    tasks = tower_weight.shape[0]
    hidden = in_weight.shape[1]
    cap = -(-(3 * tok_rows // count) // 8) * 8
    rows_all = count * cap
    chunk = 256
    chunks = hidden // chunk
    per_owner = bag_rows.shape[0] // count
    held = -(-per_owner // 8) * 8

    def bags(values, empty):
        return jnp.pad(
            values.reshape(count, per_owner), ((0, 0), (0, held - per_owner)), constant_values=empty
        )

    def rows8(values):
        return jnp.pad(values, ((0, 8 - values.shape[0]), (0, 0)))

    bag_tiles = jnp.pad(
        bag_rows.reshape(count, 1, per_owner), ((0, 0), (0, 7), (0, 128 - per_owner)), constant_values=-1
    )
    vmem = pl.BlockSpec(memory_space=pltpu.VMEM)
    anywhere = pl.BlockSpec(memory_space=pl.ANY)
    scalars = (count, 8, 128)
    routed = (count, cap, feature)
    owned = (count, held, feature)
    half_rows = hidden // 2
    in_parts, hidden_parts, small, grads, rows = pl.pallas_call(
        functools.partial(kernel, (count, cap, chunk, chunks)),
        out_shape=(
            jax.ShapeDtypeStruct((2, half_rows, feature), F32),
            jax.ShapeDtypeStruct((2, chunks // 2, 8, chunk), F32),
            jax.ShapeDtypeStruct((8, feature), F32),
            jax.ShapeDtypeStruct((2,) + owned, BF16),
            jax.ShapeDtypeStruct((2,) + scalars, jnp.int32),
        ),
        in_specs=[vmem] * 4 + [anywhere] * 2 + [vmem] * 6,
        out_specs=(vmem,) * 5,
        scratch_shapes=[
            pltpu.VMEM((hidden, feature), BF16),
            pltpu.VMEM((hidden, feature), BF16),
            pltpu.VMEM((chunks, feature, chunk), BF16),
            pltpu.VMEM((chunks, 16, chunk), BF16),
            pltpu.VMEM((hidden, 8), F32),
            pltpu.VMEM((hidden, rows_all), BF16),
            pltpu.VMEM((hidden, rows_all), F32),
            pltpu.VMEM((hidden, rows_all), BF16),
            pltpu.VMEM((rows_all, tok_rows), BF16),
            pltpu.VMEM(routed, BF16),
            pltpu.VMEM(routed, BF16),
            pltpu.VMEM(scalars, F32),
            pltpu.VMEM(scalars, F32),
            pltpu.VMEM(scalars, F32),
            pltpu.VMEM(scalars, F32),
            pltpu.VMEM(routed, BF16),
            pltpu.VMEM(routed, BF16),
            pltpu.VMEM(owned, BF16),
            pltpu.VMEM(owned, BF16),
            pltpu.VMEM(scalars, jnp.int32),
            pltpu.VMEM((count, 8, feature), F32),
            pltpu.VMEM((count, 8, feature), F32),
            pltpu.VMEM((8, feature), F32),
            pltpu.VMEM((8, feature), F32),
            pltpu.VMEM((half_rows, feature), F32),
            pltpu.VMEM((chunks // 2, 8, chunk), F32),
            pltpu.VMEM((16, rows_all), F32),
            pltpu.VMEM((feature, rows_all), F32),
            pltpu.SemaphoreType.DMA((7, count)),
            pltpu.SemaphoreType.DMA((7, count)),
            pltpu.SemaphoreType.DMA((5,)),
            pltpu.SemaphoreType.DMA((5,)),
            pltpu.SemaphoreType.DMA((2,)),
        ],
        compiler_params=pltpu.CompilerParams(
            collective_id=0, has_side_effects=True, vmem_limit_bytes=VMEM_LIMIT
        ),
    )(
        pooled,
        routes,
        rows8(routes.T),
        rows8(labels.T.astype(F32)),
        in_weight[0],
        out_weight[0],
        gate_weight.transpose(1, 0, 2),
        rows8(tower_weight),
        rows8(tower_bias[:, None]),
        bag_tiles,
        bags(bag_sample, -1).reshape(-1, 1),
        bags(bag_weight, 0.0).reshape(-1, 1),
    )
    in_grad = (in_parts[0] + in_parts[1])[None]
    hidden_sum = (hidden_parts[0] + hidden_parts[1])[:, :tasks, :]
    out_grad = sum(
        hidden_sum[:, t].reshape(-1, 1) * tower_weight[t][None, :] for t in range(tasks)
    )[None]
    owned_rows = rows[:, :, 0, :held].reshape(-1)
    matches = (
        jnp.arange(row_table.shape[0], dtype=jnp.int32)[:, None] == owned_rows[None, :]
    ).astype(BF16)
    new_table = row_table - STEP_SIZE * mm(matches, grads.reshape(-1, feature))
    return (in_grad, out_grad, small[None, tasks : 2 * tasks], small[:tasks], new_table)


def solution(mesh):
    in_specs = (
        P(("expert", "dp"), None),
        P(("expert", "dp"), None),
        P(("expert", "dp"), None),
        P("expert", None, None),
        P("expert", None, None),
        P(),
        P(),
        P(),
        P(("expert", "dp")),
        P(("expert", "dp")),
        P(("expert", "dp")),
        P("expert", None),
    )
    out_specs = (
        P("expert", "dp", None),
        P("expert", "dp", None),
        P("expert", None, None),
        P(),
        P("expert", None),
    )
    return jax.shard_map(
        on_device, mesh=mesh, in_specs=in_specs, out_specs=out_specs, check_vma=False
    )
```

time: 192 us -> 96.2 us (0.50)
  Pallas kernels: 0 us -> 73.7 us
  blocking collectives: 43 us -> 0 us
  matrix products: 38.4 us -> 1.81 us
  waiting for transfers between devices: 35.3 us -> 0 us
  starting transfers between devices: 26.6 us -> 0 us
  between operations: 14 us -> 0.7 us
  other arithmetic: 15.6 us -> 6.22 us
  local copies, waits for them, and re-layouts: 18.3 us -> 13.4 us
    pallas_call x0 -> x1, Pallas kernels: none -> 73.7 us  [on_device(): pl.pallas_call(functools.partial(kernel, (count, cap, chunk, chunks)), ou...]
    psum x2 -> x0, blocking collectives: 43 us -> none  [the longest x1 40 us: on_device(): tower_grad = lax.psum(tower_local, ('expert', 'dp'))]
    dot_general x18 -> x1, matrix products: 38.4 us -> 1.81 us  [mm(): lax.dot_general(left, right, (((left_dim,), (right_dim,)), ((), ())), pre...]
    all_to_all x6 -> x0, waiting for transfers between devices: 35.3 us -> none  [swap(): lax.all_to_all(values, 'expert', split_axis=0, concat_axis=0, tiled=True)]
    all_to_all x6 -> x0, starting transfers between devices: 26.4 us -> none  [swap(): lax.all_to_all(values, 'expert', split_axis=0, concat_axis=0, tiled=True)]
    convert_element_type x5 -> x1, other arithmetic: 8.94 us -> 0.68 us  [on_device(): labels.T.astype(F32)]
    unnamed x27 -> x12, local copies, waits for them, and re-layouts: 9.99 us -> 2.82 us
    pad x0 -> x5, local copies, waits for them, and re-layouts: none -> 4.39 us  [the longest x4 3.75 us: rows8(): return jnp.pad(values, ((0, 8 - values.shape[0]), (0, 0)))]
  transfers between devices with their start and end apart: 9 -> 0, of which waited for: 6 -> 0; matrix products, arithmetic and copies ran while one was open for 19% -> 0% of each run, Pallas kernels for 0% -> 0%
where the time goes in v2:
time: 96.2 us; the launch traced here: 95.8 us
  Pallas kernels  73.7 us (77%)
  local copies, waits for them, and re-layouts  13.4 us (14%)
  other arithmetic  6.22 us (6%)
  matrix products  1.81 us (2%)
    pallas_call x1, Pallas kernels, on_device(): pl.pallas_call(functools.partial(kernel, (count, cap, chunk, chunks)), ou...  73.7 us
    add x1, other arithmetic, on_device(): in_grad = (in_parts[0] + in_parts[1])[None]  3.85 us
    pad x4, local copies, waits for them, and re-layouts, rows8(): return jnp.pad(values, ((0, 8 - values.shape[0]), (0, 0)))  3.75 us
    unnamed x12, local copies, waits for them, and re-layouts  2.82 us

profile of v2, /device:TPU:0, one launch (start us, length us, event | category | flops | bytes accessed | tf_op | source)
XLA Modules:
  0.0 95.8 jit_solution(6685241902204502932)
XLA Ops:
  0.6 1.5 %copy.22.routes_ref = s32[256,2]{1,0:T(8,128)} copy(s32[256,2]{0,1:T(2,128)} %param.13) | data formatting | bytes 4096 | tf_op args[1]
  2.1 1.3 %pad.19.routes_rows_ref = s32[8,256]{1,0:T(8,128)} pad(s32[2,256]{1,0:T(2,128)} %bitcast.26, s32[]{:T(128)} %constant.1.clone.1), padding=0_6x0_0 | pad | bytes 10244 | tf_op jit(solution)/shard_map/jit(_pad)/pad | solution.py:402
  3.4 0.7 convert_bitcast_fusion
  4.1 0.6 pad.20.labels_ref
  4.7 1.3 %copy.26 = bf16[16,2,256]{2,0,1:T(8,128)(2,1)} copy(bf16[16,2,256]{2,1,0:T(2,128)(2,1)} %param.17) | data formatting | bytes 32768 | tf_op args[5]
  6.0 1.3 %pad.21.tower_ref = f32[8,256]{1,0:T(8,128)} pad(f32[2,256]{1,0:T(2,128)} %param.18, f32[]{:T(128)} %constant.2.clone.1), padding=0_6x0_0 | pad | bytes 10244 | tf_op jit(solution)/shard_map/jit(_pad)/pad | solution.py:402
  7.3 0.7 copy.21
  8.0 0.6 pad.22.bias_ref
  8.6 0.8 reshape.143
  9.4 0.6 pad.23.bag_rows_ref
  10.0 1.5 %copy.23.bag_sample_ref = s32[512,1]{1,0:T(8,128)} copy(s32[512,1]{0,1:T(1,128)} %bitcast.29) | data formatting | bytes 4096 | tf_op jit(solution)/shard_map/reshape | solution.py:473
  11.5 1.5 %copy.24.bag_weight_ref = f32[512,1]{1,0:T(8,128)} copy(f32[512,1]{0,1:T(1,128)} %bitcast.30) | data formatting | bytes 4096 | tf_op jit(solution)/shard_map/reshape | solution.py:474
  13.1 73.7 %shard_map.155 = (f32[2,2048,256]{2,1,0:T(8,128)}, f32[2,8,8,256]{3,2,1,0:T(8,128)}, f32[8,256]{1,0:T(8,128)}, bf16[2,16,32,256]{3,2,1,0:T(8,128)(2,1)}, s32[2,16,8,128]{3,2,1,0:T(8,128)}) custom-call(bf16[256,256]{1,0:T(8,128)(2,1)} %pooled_ref.1, s32[256,2]{1,0:T(8,128)} %copy.22.routes_ref, s32[8,256]{1,0:T(8,128)} %pad.19.routes_rows_ref, ...), custom_call_target="tpu_custom_call" | custom-call | tf_op jit(solution)/shard_map/pallas_call | solution.py:413
  86.8 0.0 copy-start.1
  86.8 0.0 copy-start
  86.8 3.8 %slice_add_fusion = f32[1,2048,256]{2,1,0:T(8,128)} fusion(f32[2,2048,256]{2,1,0:T(8,128)} %get-tuple-element.10), kind=kLoop, calls=%fused_computation.4 | loop fusion | flops 524288 | bytes 6291456 | tf_op jit(solution)/shard_map/add | solution.py:476
  90.6 0.0 copy-done.1
  90.6 0.0 copy-start.2
  90.6 0.0 copy-start.3
  90.6 0.0 copy-start.4
  90.7 0.0 copy-done
  90.7 1.7 %multiply_add_fusion = f32[1,2048,256]{2,1,0:T(8,128)} fusion(f32[256]{0:T(256)S(1)} %bitcast.28, f32[2048]{0:T(1024)S(1)} %bitcast.25, f32[256]{0:T(256)S(1)} %bitcast.27, f32[2048]{0:T(1024)S(1)} %bitcast.24), kind=kLoop, calls=%fused_computation.3 | loop fusion | flops 1572864 | bytes 2115584 | tf_op jit(solution)/shard_map/add | solution.py:478
  92.4 0.0 copy-done.2
  92.4 0.6 fusion.5
  93.0 0.9 slice_reduce_fusion
  93.9 0.1 eq.16
  94.0 0.0 copy-done.3
  94.0 0.0 copy-done.4
  94.0 1.8 %fusion.3 = f32[1024,256]{1,0:T(8,128)} fusion(f32[1024,256]{1,0:T(8,128)S(1)} %copy-done.3, bf16[1024,256]{1,0:T(8,128)(2,1)S(1)} %bitcast.31, s32[1024]{0:T(1024)S(1)} %eq.16), kind=kOutput, calls=%fused_computation.6 | convolution fusion | flops 538443776 | bytes 2625536 | tf_op jit(solution)/shard_map/dot_general | solution.py:18
  (3 shorter events, 0.0 us)
Async XLA Ops:
  86.8 3.9 %copy-start.1 = (f32[2,256]{1,0:T(2,128)S(1)}, f32[2,256]{1,0:T(2,128)}, u32[]{:S(2)}) copy-start(f32[2,256]{1,0:T(2,128)} %param.18) | copy-start | bytes 6148
  86.8 3.9 %copy-start = (f32[2,8,8,256]{3,2,1,0:T(8,128)S(1)}, f32[2,8,8,256]{3,2,1,0:T(8,128)}, u32[]{:S(2)}) copy-start(f32[2,8,8,256]{3,2,1,0:T(8,128)} %get-tuple-element.11) | copy-start | bytes 393220
  90.6 1.7 %copy-start.2 = (f32[8,256]{1,0:T(8,128)S(1)}, f32[8,256]{1,0:T(8,128)}, u32[]{:S(2)}) copy-start(f32[8,256]{1,0:T(8,128)} %get-tuple-element.12) | copy-start | bytes 24580
  90.6 3.4 %copy-start.3 = (f32[1024,256]{1,0:T(8,128)S(1)}, f32[1024,256]{1,0:T(8,128)}, u32[]{:S(2)}) copy-start(f32[1024,256]{1,0:T(8,128)} %param.23) | copy-start | bytes 3145732
  90.6 3.4 %copy-start.4 = (bf16[2,16,32,256]{3,2,1,0:T(8,128)(2,1)S(1)}, bf16[2,16,32,256]{3,2,1,0:T(8,128)(2,1)}, u32[]{:S(2)}) copy-start(bf16[2,16,32,256]{3,2,1,0:T(8,128)(2,1)} %get-tuple-element.14) | copy-start | bytes 1572868

commit v3 on v2

--- a/solution.py
+++ b/solution.py
@@ -84,7 +84,6 @@
 def kernel(
     sizes,
     pooled_ref,
-    routes_ref,
     routes_rows_ref,
     labels_ref,
     in_hbm,
@@ -95,7 +94,8 @@
     bag_rows_ref,
     bag_sample_ref,
     bag_weight_ref,
-    in_parts_ref,
+    in_mine_hbm,
+    in_recv_hbm,
     hidden_parts_ref,
     small_ref,
     grads_ref,
@@ -119,11 +119,13 @@
     d_recv,
     e_send,
     e_recv,
+    r_send,
     r_recv,
     t_send,
     t_recv,
     s_send,
     s_recv,
+    in_mine,
     in_other,
     hidden_other,
     rows_acc,
@@ -134,7 +136,7 @@
     dp_recv,
     local_sem,
 ):
-    count, cap, chunk, chunks = sizes
+    count, cap, chunk, chunks, per_owner = sizes
     rows_all = count * cap
     tok_rows = pooled_ref.shape[0]
     me, core = lax.axis_index("expert"), lax.axis_index("dp")
@@ -149,7 +151,7 @@
     c_start, c_wait, c_drain = phase(2, c_send, c_recv)
     d_start, d_wait, d_drain = phase(3, d_send, d_recv)
     e_start, e_wait, e_drain = phase(4, e_send, e_recv)
-    r_start, r_wait, r_drain = phase(5, bag_rows_ref, r_recv)
+    r_start, r_wait, r_drain = phase(5, r_send, r_recv)
     t_start, t_wait, t_drain = phase(6, t_send, t_recv)
 
     def to_other(index, source, target):
@@ -193,6 +195,14 @@
     fill = one_hot((places == first_slot) | (places == second_slot)).astype(BF16)
     place_ref[...] = fill
     a_send[...] = mm(fill, pooled_ref[...]).astype(BF16).reshape(a_send.shape)
+
+    @pl.loop(0, count)
+    def _(owner):
+        line = bag_rows_ref[pl.ds(owner * per_owner // 128, 1), :]
+        shift = lax.rem(128 - lax.rem(owner * per_owner, 128), 128)
+        line = pltpu.roll(jnp.broadcast_to(line, (8, 128)), shift, 1)
+        r_send[owner] = jnp.where(iota((8, 128), 1) < per_owner, line, -1)
+
     pl.semaphore_wait(barrier, count)
     a_start()
     r_start()
@@ -202,15 +212,28 @@
     second_at = one_hot(lanes == second_rank.astype(jnp.int32)).astype(BF16)
     signed = first_map - second_map
     row_of = iota((8, tok_rows), 0)
+    labels = jnp.where(row_of == 0, labels_ref[0:1, :], labels_ref[1:2, :]).astype(F32)
+    bias = jnp.where(row_of == 0, bias_ref[0], bias_ref[1])
+    gates = [gate_ref[:, task, :] for task in range(2)]
+    feat_row = iota((8, tower_ref.shape[1]), 0)
+    tower_rows = jnp.where(
+        feat_row == 0, tower_ref[0:1, :], jnp.where(feat_row == 1, tower_ref[1:2, :], 0.0)
+    )
+    sample_wide = jnp.broadcast_to(bag_sample_ref[...].astype(F32), (8, bag_sample_ref.shape[1]))
+    weight_wide = jnp.broadcast_to(bag_weight_ref[...], (8, bag_sample_ref.shape[1]))
+    sample_col, weight_col = sample_wide.T[:, 0:1], weight_wide.T[:, 0:1]
+    bag = one_hot(
+        iota((bag_sample_ref.shape[1], tok_rows), 1) == sample_col.astype(jnp.int32)
+    ).astype(BF16)
     gate_logit = jnp.zeros((8, tok_rows), F32)
     for task in range(2):
-        logits = nt(gate_ref[task], pooled_ref[...])
+        logits = nt(gates[task], pooled_ref[...])
         gate_logit = jnp.where(
             row_of == task, jnp.sum(signed * logits, axis=0, keepdims=True), gate_logit
         )
     gate_first = sigmoid(gate_logit)
     gate_second = 1.0 - gate_first
-    tower_high, tower_low = halves(tower_ref[...])
+    tower_high, tower_low = halves(tower_rows)
     tower_high, tower_low = tower_high.astype(BF16), tower_low.astype(BF16)
     load_out.wait()
     load_in.wait()
@@ -230,10 +253,11 @@
     def _(step):
         span = pl.ds(pl.multiple_of(step * chunk, chunk), chunk)
         before = nt(in_ref[span, :], a_recv[...].reshape(rows_all, -1))
-        sigma = sigmoid(before)
-        act = before * sigma
-        slope_ref[span, :] = (sigma + act * (1.0 - sigma)).astype(slope_ref.dtype)
-        act = act.astype(BF16)
+        near = 0.5 * before
+        bend = jnp.tanh(near)
+        bent = near * bend
+        slope_ref[span, :] = (1.0 + bend) + (near - bent * bend)
+        act = (near + bent).astype(BF16)
         act_ref[span, :] = act
         rows_acc[...] += mm(proj_rows_ref[step], act)
 
@@ -257,8 +281,8 @@
         return jnp.sum((mask * found).reshape(count, 8, tok_rows), axis=0)
 
     first_dot, second_dot = pick(first_mask, first_at), pick(second_mask, second_at)
-    task_logit = gate_first * first_dot + gate_second * second_dot + bias_ref[...]
-    logit_grad = LOSS_SCALE * (sigmoid(task_logit) - labels_ref[...])
+    task_logit = gate_first * first_dot + gate_second * second_dot + bias
+    logit_grad = LOSS_SCALE * (sigmoid(task_logit) - labels)
     first_grad = logit_grad * (first_dot - second_dot) * gate_first * gate_second
     lower = pltpu.roll(first_grad, 2, 0)
     keep = row_of < 4
@@ -277,7 +301,7 @@
     gate_input = jnp.zeros((tok_rows, pooled_ref.shape[1]), F32)
     for task in range(2):
         high, low = halves(signed * first_grad[task : task + 1, :])
-        weights = gate_ref[task]
+        weights = gates[task]
         gate_input += mm(high.astype(BF16), weights, 0, 0) + mm(low.astype(BF16), weights, 0, 0)
     c_wait()
     coefs = jnp.zeros((8, rows_all), F32)
@@ -289,7 +313,7 @@
         )
 
     coefs = lax.fori_loop(0, count, place, coefs)
-    coef_zero, coef_one = coefs[0:1, :], coefs[1:2, :]
+    coef_zero, coef_one = 0.5 * coefs[0:1, :], 0.5 * coefs[1:2, :]
     back_acc[...] = jnp.zeros_like(back_acc)
 
     @pl.loop(0, chunks)
@@ -297,7 +321,7 @@
         span = pl.ds(pl.multiple_of(step * chunk, chunk), chunk)
         cols = proj_cols_ref[span, :]
         hidden_grad = cols[:, 0:1] * coef_zero + cols[:, 1:2] * coef_one
-        grad = (hidden_grad * slope_ref[span, :].astype(F32)).astype(BF16)
+        grad = (hidden_grad * slope_ref[span, :]).astype(BF16)
         pre_ref[span, :] = grad
         back_acc[...] += mm(turned_ref[step], grad)
 
@@ -322,37 +346,34 @@
         lambda i, total: total + weight_chunk(other * half + i, in_other, hidden_other, i),
         tower,
     )
-    in_copy = to_other(0, in_other, in_parts_ref.at[1])
+    in_copy = to_other(0, in_other, in_recv_hbm)
     hidden_copy = to_other(1, hidden_other, hidden_parts_ref.at[1])
     in_copy.start()
     hidden_copy.start()
-    d_wait()
-    pooled_grad = gate_input + mm(
-        place_ref[...], d_recv[...].reshape(rows_all, -1), 0, 0
-    )
-    bag = one_hot(iota((bag_sample_ref.shape[0], tok_rows), 1) == bag_sample_ref[...]).astype(BF16)
-    high, low = halves(pooled_grad)
-    bag_grad = mm(bag, high.astype(BF16)) + mm(bag, low.astype(BF16))
-    e_send[...] = (bag_weight_ref[...] * bag_grad).astype(BF16).reshape(e_send.shape)
-    e_start()
     tower = lax.fori_loop(
         0,
         half,
         lambda i, total: total
-        + weight_chunk(core * half + i, in_parts_ref.at[0], hidden_parts_ref.at[0], i),
+        + weight_chunk(core * half + i, in_mine, hidden_parts_ref.at[0], i),
         tower,
     )
     gate = folded(mm(coef_rows, a_recv[...].reshape(rows_all, -1)))
     tile = jnp.where(iota(tower.shape, 0) < 2, tower, gate)
     t_send[...] = jnp.broadcast_to(tile[None], t_send.shape)
     t_start()
+    store_in = pltpu.make_async_copy(in_mine, in_mine_hbm, local_sem.at[0])
+    store_in.start()
+    d_wait()
+    pooled_grad = gate_input + mm(
+        place_ref[...], d_recv[...].reshape(rows_all, -1), 0, 0
+    )
+    high, low = halves(pooled_grad)
+    bag_grad = mm(bag, high.astype(BF16)) + mm(bag, low.astype(BF16))
+    e_send[...] = (weight_col * bag_grad).astype(BF16).reshape(e_send.shape)
+    e_start()
     r_wait()
-    e_wait()
-    grads_copy = to_other(2, e_recv, grads_ref.at[core])
     rows_copy = to_other(3, r_recv, rows_ref.at[core])
-    grads_copy.start()
     rows_copy.start()
-    grads_ref[core] = e_recv[...]
     rows_ref[core] = r_recv[...]
     t_wait()
     summed = lax.fori_loop(0, count, lambda i, total: total + t_recv[i], jnp.zeros_like(tower))
@@ -360,9 +381,14 @@
     s_send[...] = mine
     small_copy = to_other(4, s_send, s_recv)
     small_copy.start()
+    e_wait()
+    grads_copy = to_other(2, e_recv, grads_ref.at[core])
+    grads_copy.start()
+    grads_ref[core] = e_recv[...]
     small_copy.wait()
     small_ref[...] = mine + s_recv[...]
-    for copy in (in_copy, hidden_copy, grads_copy, rows_copy):
+    store_in.wait()
+    for copy in (in_copy, hidden_copy, rows_copy, grads_copy):
         copy.wait()
     for drain in (a_drain, b_drain, c_drain, d_drain, e_drain, r_drain, t_drain):
         drain()
@@ -388,39 +414,40 @@
     hidden = in_weight.shape[1]
     cap = -(-(3 * tok_rows // count) // 8) * 8
     rows_all = count * cap
-    chunk = 256
+    chunk = 1024 if rows_all * 1024 < 2**20 else 512
     chunks = hidden // chunk
     per_owner = bag_rows.shape[0] // count
     held = -(-per_owner // 8) * 8
 
     def bags(values, empty):
+        if held == per_owner:
+            return values
         return jnp.pad(
             values.reshape(count, per_owner), ((0, 0), (0, held - per_owner)), constant_values=empty
         )
 
-    def rows8(values):
-        return jnp.pad(values, ((0, 8 - values.shape[0]), (0, 0)))
-
-    bag_tiles = jnp.pad(
-        bag_rows.reshape(count, 1, per_owner), ((0, 0), (0, 7), (0, 128 - per_owner)), constant_values=-1
-    )
     vmem = pl.BlockSpec(memory_space=pltpu.VMEM)
     anywhere = pl.BlockSpec(memory_space=pl.ANY)
     scalars = (count, 8, 128)
     routed = (count, cap, feature)
     owned = (count, held, feature)
     half_rows = hidden // 2
-    in_parts, hidden_parts, small, grads, rows = pl.pallas_call(
-        functools.partial(kernel, (count, cap, chunk, chunks)),
+    in_mine, in_other, hidden_parts, small, grads, rows = pl.pallas_call(
+        functools.partial(kernel, (count, cap, chunk, chunks, per_owner)),
         out_shape=(
-            jax.ShapeDtypeStruct((2, half_rows, feature), F32),
+            jax.ShapeDtypeStruct((half_rows, feature), F32),
+            jax.ShapeDtypeStruct((half_rows, feature), F32),
             jax.ShapeDtypeStruct((2, chunks // 2, 8, chunk), F32),
             jax.ShapeDtypeStruct((8, feature), F32),
             jax.ShapeDtypeStruct((2,) + owned, BF16),
             jax.ShapeDtypeStruct((2,) + scalars, jnp.int32),
         ),
-        in_specs=[vmem] * 4 + [anywhere] * 2 + [vmem] * 6,
-        out_specs=(vmem,) * 5,
+        in_specs=[vmem] * 3
+        + [anywhere] * 2
+        + [vmem] * 2
+        + [pl.BlockSpec(memory_space=pltpu.SMEM)]
+        + [vmem] * 3,
+        out_specs=(anywhere,) * 2 + (vmem,) * 4,
         scratch_shapes=[
             pltpu.VMEM((hidden, feature), BF16),
             pltpu.VMEM((hidden, feature), BF16),
@@ -442,10 +469,12 @@
             pltpu.VMEM(owned, BF16),
             pltpu.VMEM(owned, BF16),
             pltpu.VMEM(scalars, jnp.int32),
+            pltpu.VMEM(scalars, jnp.int32),
             pltpu.VMEM((count, 8, feature), F32),
             pltpu.VMEM((count, 8, feature), F32),
             pltpu.VMEM((8, feature), F32),
             pltpu.VMEM((8, feature), F32),
+            pltpu.VMEM((half_rows, feature), F32),
             pltpu.VMEM((half_rows, feature), F32),
             pltpu.VMEM((chunks // 2, 8, chunk), F32),
             pltpu.VMEM((16, rows_all), F32),
@@ -461,19 +490,18 @@
         ),
     )(
         pooled,
-        routes,
-        rows8(routes.T),
-        rows8(labels.T.astype(F32)),
+        routes.T,
+        labels.T,
         in_weight[0],
         out_weight[0],
-        gate_weight.transpose(1, 0, 2),
-        rows8(tower_weight),
-        rows8(tower_bias[:, None]),
-        bag_tiles,
-        bags(bag_sample, -1).reshape(-1, 1),
-        bags(bag_weight, 0.0).reshape(-1, 1),
-    )
-    in_grad = (in_parts[0] + in_parts[1])[None]
+        gate_weight,
+        tower_weight,
+        tower_bias,
+        bag_rows.reshape(-1, 128),
+        bags(bag_sample, -1).reshape(1, -1),
+        bags(bag_weight, 0.0).reshape(1, -1),
+    )
+    in_grad = (in_mine + in_other)[None]
     hidden_sum = (hidden_parts[0] + hidden_parts[1])[:, :tasks, :]
     out_grad = sum(
         hidden_sum[:, t].reshape(-1, 1) * tower_weight[t][None, :] for t in range(tasks)

time: 96.2 us -> 76.1 us (0.79)
  local copies, waits for them, and re-layouts: 13.4 us -> 1.64 us
  Pallas kernels: 73.7 us -> 66.2 us
    pallas_call x1, Pallas kernels: 73.7 us -> 66.2 us  [on_device(): pl.pallas_call(functools.partial(kernel, (count, cap, chunk, chunks, per_...]
    pad x5 -> x0, local copies, waits for them, and re-layouts: 4.39 us -> none  [the longest x4 3.75 us: rows8(): return jnp.pad(values, ((0, 8 - values.shape[0]), (0, 0)))]
    add x1 -> x0, other arithmetic: 3.85 us -> none  [on_device(): in_grad = (in_parts[0] + in_parts[1])[None]]
    broadcast_in_dim x0 -> x1, other arithmetic: none -> 3.85 us  [on_device(): in_grad = (in_mine + in_other)[None]]
    reshape x3 -> x0, local copies, waits for them, and re-layouts: 3.83 us -> none  [the longest x1 1.53 us: on_device(): bags(bag_sample, -1).reshape(-1, 1)]
    unnamed x12 -> x10, local copies, waits for them, and re-layouts: 2.82 us -> 0.02 us
where the time goes in v3:
time: 76.1 us; the launch traced here: 75.9 us
  Pallas kernels  66.2 us (87%)
  other arithmetic  5.53 us (7%)
  matrix products  1.81 us (2%)
  local copies, waits for them, and re-layouts  1.64 us (2%)
    pallas_call x1, Pallas kernels, on_device(): pl.pallas_call(functools.partial(kernel, (count, cap, chunk, chunks, per_...  66.2 us
    broadcast_in_dim x1, other arithmetic, on_device(): in_grad = (in_mine + in_other)[None]  3.85 us
    dot_general x1, matrix products, mm(): lax.dot_general(left, right, (((left_dim,), (right_dim,)), ((), ())), pre...  1.81 us
    add x1, other arithmetic, on_device(): sum((hidden_sum[:, t].reshape(-1, 1) * tower_weight[t][None, :] for t in...  1.68 us

profile of v3, /device:TPU:0, one launch (start us, length us, event | category | flops | bytes accessed | tf_op | source)
XLA Modules:
  0.0 75.9 jit_solution(3881921973833604883)
XLA Ops:
  0.6 66.2 %shard_map.155 = (f32[2048,256]{1,0:T(8,128)}, f32[2048,256]{1,0:T(8,128)}, f32[2,2,8,1024]{3,2,1,0:T(8,128)}, f32[8,256]{1,0:T(8,128)}, bf16[2,16,32,256]{3,2,1,0:T(8,128)(2,1)}, /*index=5*/s32[2,16,8,128]{3,2,1,0:T(8,128)}) custom-call(bf16[256,256]{1,0:T(8,128)(2,1)} %pooled_ref.1, s32[2,256]{1,0:T(2,128)} %bitcast.25, s32[2,256]{1,0:T(2,128)} %bitcast.26, ...), custom_call_target="tpu_custom_call" | custom-call | tf_op jit(solution)/shard_map/pallas_call | solution.py:435
  66.9 0.0 copy-start.1
  66.9 0.0 copy-start
  66.9 3.8 %add_bitcast_fusion = f32[1,2048,256]{2,1,0:T(8,128)} fusion(f32[2048,256]{1,0:T(8,128)} %get-tuple-element.11, f32[2048,256]{1,0:T(8,128)} %get-tuple-element.12), kind=kLoop, calls=%fused_computation.4 | loop fusion | flops 524288 | bytes 6291456 | tf_op jit(solution)/shard_map/broadcast_in_dim | solution.py:504
  70.7 0.0 copy-done.1
  70.7 0.0 copy-start.2
  70.7 0.0 copy-start.3
  70.7 0.0 copy-start.4
  70.8 0.0 copy-done
  70.8 1.7 %multiply_add_fusion = f32[1,2048,256]{2,1,0:T(8,128)} fusion(f32[256]{0:T(256)S(1)} %bitcast.24, f32[2048]{0:T(1024)S(1)} %bitcast.22, f32[256]{0:T(256)S(1)} %bitcast.23, f32[2048]{0:T(1024)S(1)} %bitcast.21), kind=kLoop, calls=%fused_computation.3 | loop fusion | flops 1572864 | bytes 2115584 | tf_op jit(solution)/shard_map/add | solution.py:506
  72.5 0.0 copy-done.2
  72.5 0.6 fusion.5
  73.1 0.9 %slice_reduce_fusion = s32[2,16,32]{2,1,0:T(8,128)S(1)} fusion(s32[2,16,8,128]{3,2,1,0:T(8,128)} %get-tuple-element.15), kind=kLoop, calls=%fused_computation.8 | loop fusion | bytes 8192 | tf_op jit(solution)/shard_map/slice | solution.py:509
  74.0 0.1 eq.16
  74.1 0.0 copy-done.3
  74.1 0.0 copy-done.4
  74.1 1.8 %fusion.3 = f32[1024,256]{1,0:T(8,128)} fusion(f32[1024,256]{1,0:T(8,128)S(1)} %copy-done.3, bf16[1024,256]{1,0:T(8,128)(2,1)S(1)} %bitcast.30, s32[1024]{0:T(1024)S(1)} %eq.16), kind=kOutput, calls=%fused_computation.6 | convolution fusion | flops 538443776 | bytes 2625536 | tf_op jit(solution)/shard_map/dot_general | solution.py:18
  (3 shorter events, 0.0 us)
Async XLA Ops:
  66.9 3.9 %copy-start.1 = (f32[2,256]{1,0:T(2,128)S(1)}, f32[2,256]{1,0:T(2,128)}, u32[]{:S(2)}) copy-start(f32[2,256]{1,0:T(2,128)} %tower_ref.1) | copy-start | bytes 6148
  66.9 3.9 %copy-start = (f32[2,2,8,1024]{3,2,1,0:T(8,128)S(1)}, f32[2,2,8,1024]{3,2,1,0:T(8,128)}, u32[]{:S(2)}) copy-start(f32[2,2,8,1024]{3,2,1,0:T(8,128)} %get-tuple-element.13) | copy-start | bytes 393220
  70.7 1.7 %copy-start.2 = (f32[8,256]{1,0:T(8,128)S(1)}, f32[8,256]{1,0:T(8,128)}, u32[]{:S(2)}) copy-start(f32[8,256]{1,0:T(8,128)} %get-tuple-element.14) | copy-start | bytes 24580
  70.7 3.4 %copy-start.3 = (f32[1024,256]{1,0:T(8,128)S(1)}, f32[1024,256]{1,0:T(8,128)}, u32[]{:S(2)}) copy-start(f32[1024,256]{1,0:T(8,128)} %param.23) | copy-start | bytes 3145732
  70.7 3.4 %copy-start.4 = (bf16[2,16,32,256]{3,2,1,0:T(8,128)(2,1)S(1)}, bf16[2,16,32,256]{3,2,1,0:T(8,128)(2,1)}, u32[]{:S(2)}) copy-start(bf16[2,16,32,256]{3,2,1,0:T(8,128)(2,1)} %get-tuple-element.16) | copy-start | bytes 1572868
